TPU v7x, 256 devices: a whole 4x4x8 slice. The times are simulated.
256 devices in a mesh: grp: 2 (over core), gx: 16 (over y, x), gy: 8 (over z).
Axes of the slice: x: 4, y: 4, z: 8, core: 2. Of those that a mesh axis runs over, the one named last changes fastest.
Arguments:
- fluxes: float32 [2, 10, 262144], P('grp', None, ('gx', 'gy')), may hold values from -6 to 6
- weights: bfloat16 [2, 64, 4096, 1024], P('grp', None, 'gx', 'gy'), may hold values from 0.049804688 to 1
- land_rows: int32 [2, 4096, 512], P('grp', 'gx', 'gy'), may hold values from 0 to 2047
- owners: int32 [2, 16, 8, 256, 1], P('grp', 'gx', 'gy'), may hold values from 0 to 127; in each aligned block of 256 rows (0 to 255, 256 to 511, ..., all dimensions but the last counted through in order) at most 4 rows name the same one
- elev_class: int32 [2, 4096, 1024], P('grp', 'gx', 'gy'), may hold values from 0 to 9
- ice_mask: int32 [2, 4096, 1024], P('grp', 'gx', 'gy'), may hold values 0 or 1
- bed: float32 [2, 4096, 1024], P('grp', 'gx', 'gy'), may hold values from -0.5 to 1
- thickness: float32 [2, 4096, 1024], P('grp', 'gx', 'gy'), may hold values from 0 to 2
- diffusivity: float32 [2, 4096, 1024], P('grp', 'gx', 'gy'), may hold values from 0.02 to 0.24
Outputs:
- land_fields: float32 [2, 2, 262144], P('grp', None, ('gx', 'gy'))
- thickness_new: float32 [2, 4096, 1024], P('grp', 'gx', 'gy')
Inputs may be any that keep to these rules, and one draw needn't show every extreme that they name: `owners`: within each ice device's 256 rows no land owner is named by more than 4 rows, a bound that some block reaches.
All inputs are finite; a program needn't handle non-finite values. No bound on the sum of `ice_mask` on one device may be relied on, other than what follows from the above.
Results may differ from a plain program's by a relative error of at most 0.00051.
Values may be sent and summed in bfloat16 or wider, within the bound.
No kernel may reach another device: no remote copies, remote signals or barrier semaphores. Data moves between devices by JAX's collectives and lax.ppermute only.
A program may use at most 64 MiB of HBM per device.

v0:
```python
import math

import jax
import jax.numpy as jnp
from jax import lax
from jax.sharding import PartitionSpec as P

STEPS = 4


SMB_RATE = 0.5
FULL_PRECISION = lax.Precision.HIGHEST


def shifted(value, axis, steps):
    count = lax.axis_size(axis)
    initial, last = (max(0, -steps), min(count, count - steps))
    return lax.ppermute(value, axis, [(source, source + steps) for source in range(initial, last)])


def padded_2(block, sides, width):
    for axis, dim in sides:
        count = lax.axis_size(axis)
        forward = [(i, i + 1) for i in range(count - 1)]
        backward = [(target, source) for source, target in forward]
        low = lax.ppermute(
            lax.slice_in_dim(block, block.shape[dim] - width, None, axis=dim), axis, forward
        )
        high = lax.ppermute(lax.slice_in_dim(block, 0, width, axis=dim), axis, backward)
        block = jnp.concatenate([low, block, high], axis=dim)
    return block


def relax_step(thick_pad, bed_pad, diff_pad, source, inside):
    surface = bed_pad + thick_pad
    centre_surface = surface[1:-1, 1:-1]
    centre_diff = diff_pad[1:-1, 1:-1]
    change = jnp.zeros_like(centre_surface)
    neighbours = (
        (surface[2:, 1:-1], diff_pad[2:, 1:-1]),
        (surface[:-2, 1:-1], diff_pad[:-2, 1:-1]),
        (surface[1:-1, 2:], diff_pad[1:-1, 2:]),
        (surface[1:-1, :-2], diff_pad[1:-1, :-2]),
    )
    for near_surface, near_diff in neighbours:
        change = change + 0.5 * (centre_diff + near_diff) * (near_surface - centre_surface)
    return jnp.maximum(thick_pad[1:-1, 1:-1] + change + SMB_RATE * source, 0.0) * inside


def pick_cells(table, index_flat, block_size):
    cell_count = table.shape[1]

    def pick_one_block(index_block):
        onehot = (
            lax.broadcasted_iota(jnp.int32, (cell_count, block_size), 0) == index_block[None, :]
        )
        return jnp.dot(
            table, onehot.astype(jnp.bfloat16), preferred_element_type=jnp.float32
        ).astype(jnp.bfloat16)

    picked = lax.map(pick_one_block, index_flat.reshape(-1, block_size))
    return jnp.transpose(picked, (1, 0, 2)).reshape(table.shape[0], -1)


def add_cells(values, index_flat, cell_count, block_size):
    value_blocks = jnp.transpose(values.reshape(values.shape[0], -1, block_size), (1, 0, 2))
    index_blocks = index_flat.reshape(-1, block_size)

    def add_one_block(total, inputs):
        value_block, index_block = inputs
        onehot = index_block[:, None] == lax.broadcasted_iota(
            jnp.int32, (block_size, cell_count), 1
        )
        total = total + jnp.dot(
            value_block,
            onehot.astype(jnp.float32),
            precision=FULL_PRECISION,
            preferred_element_type=jnp.float32,
        )
        return (total, None)

    start = jnp.zeros((values.shape[0], cell_count), jnp.float32)
    total, unused = lax.scan(add_one_block, start, (value_blocks, index_blocks))
    return total


def per_device(
    fluxes, weights, land_rows, owners, elev_class, ice_mask, bed, thickness, diffusivity
):
    rows_gx = lax.axis_size("gx")
    cols_gy = lax.axis_size("gy")
    groups = rows_gx * cols_gy
    land_half = fluxes[0].astype(jnp.bfloat16)
    block_weights = weights[0]
    local_rows = land_rows[0]
    owner_list = owners[0, 0, 0, :, 0]
    row_count = owner_list.shape[0]
    block_width = local_rows.shape[1]
    cell_count = land_half.shape[1]
    class_count = land_half.shape[0]
    capacity = 2 * row_count // groups
    slot_total = groups * capacity
    row_iota = jnp.arange(row_count, dtype=jnp.int32)
    earlier_same = (owner_list[:, None] == owner_list[None, :]) & (
        row_iota[None, :] < row_iota[:, None]
    )
    slot_rank = jnp.sum(earlier_same.astype(jnp.int32), axis=1)
    slot_index = owner_list * capacity + slot_rank
    placement = slot_index[:, None] == jnp.arange(slot_total, dtype=jnp.int32)[None, :]
    place_float = placement.astype(jnp.float32)
    place_half = placement.astype(jnp.bfloat16)
    wanted = jnp.dot(
        place_float.T,
        local_rows.astype(jnp.float32),
        precision=FULL_PRECISION,
        preferred_element_type=jnp.float32,
    ).astype(jnp.int32)
    wanted = wanted.reshape(groups, capacity * block_width)
    wanted = shifted(wanted, "grp", -1)
    asked_rows = lax.all_to_all(wanted, ("gx", "gy"), split_axis=0, concat_axis=0, tiled=True)
    asked_flat = asked_rows.reshape(-1)
    block_size = math.gcd(asked_flat.shape[0], 2048)
    answer = pick_cells(land_half, asked_flat, block_size).reshape(
        class_count, groups, capacity * block_width
    )
    answer = lax.all_to_all(answer, ("gx", "gy"), split_axis=1, concat_axis=1, tiled=True)
    answer = shifted(answer, "grp", 1)
    answer = answer.reshape(class_count, slot_total, block_width)
    picked_half = jnp.einsum(
        "esb,rs->erb", answer, place_half, preferred_element_type=jnp.float32
    ).astype(jnp.bfloat16)
    weight_total = jnp.sum(block_weights, axis=0, dtype=jnp.float32)
    remapped = (
        jnp.einsum("erb,brj->erj", picked_half, block_weights, preferred_element_type=jnp.float32)
        / weight_total
    )
    keep_mask = ice_mask[0].astype(jnp.float32)
    class_level = jnp.arange(class_count, dtype=jnp.int32)[:, None, None]
    source = keep_mask * jnp.sum(
        jnp.where(elev_class[0][None] == class_level, remapped, 0.0), axis=0
    )
    bed_local = bed[0]
    diff_local = diffusivity[0]
    thick_now = thickness[0]
    static_pad = padded_2(jnp.stack([bed_local, diff_local]), (("gx", 1), ("gy", 2)), 1)
    for sweep in range(STEPS):
        padded = padded_2(thick_now, (("gx", 0), ("gy", 1)), 1)
        thick_now = relax_step(padded, static_pad[0], static_pad[1], source, 1.0)
    surface = bed_local + thick_now
    ice_fraction = keep_mask * jnp.minimum(thick_now, 1.0)
    fields = (jnp.stack([surface, ice_fraction, jnp.ones_like(surface)]) / weight_total).astype(
        jnp.bfloat16
    )
    partial_value = jnp.einsum(
        "brj,qrj->qrb", block_weights, fields, preferred_element_type=jnp.float32
    )
    outgoing = jnp.einsum(
        "qrb,rs->qsb",
        partial_value,
        place_float,
        precision=FULL_PRECISION,
        preferred_element_type=jnp.float32,
    )
    outgoing = outgoing.reshape(3, groups, capacity * block_width)
    outgoing = shifted(outgoing, "grp", -1)
    arrived = lax.all_to_all(outgoing, ("gx", "gy"), split_axis=1, concat_axis=1, tiled=True)
    land_sums = add_cells(arrived.reshape(3, -1), asked_flat, cell_count, block_size)
    averaged = land_sums[:2] / jnp.maximum(land_sums[2], 1.0)
    is_land = lax.axis_index("grp") == 0
    land_fields = jnp.where(is_land, averaged, 0.0)[None]
    thickness_new = jnp.where(is_land, 0.0, thick_now)[None]
    return (land_fields, thickness_new)


def solution(mesh):
    return jax.shard_map(
        per_device,
        mesh=mesh,
        in_specs=(
            P("grp", None, ("gx", "gy")),
            P("grp", None, "gx", "gy"),
            P("grp", "gx", "gy"),
            P("grp", "gx", "gy", None, None),
            P("grp", "gx", "gy"),
            P("grp", "gx", "gy"),
            P("grp", "gx", "gy"),
            P("grp", "gx", "gy"),
            P("grp", "gx", "gy"),
        ),
        out_specs=(P("grp", None, ("gx", "gy")), P("grp", "gx", "gy")),
        check_vma=False,
    )
```

profile of v0, /device:TPU:1, one launch (start us, length us, event | category | flops | bytes accessed | tf_op | source)
XLA Modules:
  0.0 331.4 jit_solution(13155291552248293725)
XLA Ops:
  3.7 5.1 %collective-permute-start.8 = (s32[128,256]{1,0:T(8,128)S(1)}, s32[128,256]{1,0:T(8,128)S(1)}, u32[]{:S(2)}, u32[]{:S(2)}) collective-permute-start(s32[128,256]{1,0:T(8,128)S(1)} %reshape.34), channel_id=1, source_target_pairs={{128,0},{129,1},{130,2},{131,3},{132,4},{133,5},{134,6},{135,7},{1... | collective-permute-start | bytes 393224 | tf_op jit(solution)/shard_map/ppermute | solution.py:18
  10.6 13.8 %all-to-all-start = ((s32[128,1,256]{2,1,0:T(1,128)}), s32[128,1,256]{2,1,0:T(1,128)S(1)}, u32[]{:S(2)}, u32[]{:S(2)}) async-start(s32[128,1,256]{2,1,0:T(1,128)} %copy.52), calls=%async_computation | async-start | bytes 262144 | tf_op jit(solution)/shard_map/all_to_all | solution.py:120
  26.3 9.6 %all-to-all-done = s32[128,1,256]{2,1,0:T(1,128)S(1)} async-done(((s32[128,1,256]{2,1,0:T(1,128)}), s32[128,1,256]{2,1,0:T(1,128)S(1)}, u32[]{:S(2)}, u32[]{:S(2)}) %all-to-all-start) | async-done | bytes 131104 | tf_op jit(solution)/shard_map/all_to_all | solution.py:120
  36.2 41.7 %while.21 = (s32[]{:T(128)}, bf16[16,10,2048]{2,1,0:T(8,128)(2,1)S(1)}, s32[16,2048]{1,0:T(8,128)S(1)}, bf16[10,2048]{1,0:T(8,128)(2,1)S(1)}, s32[]{:T(128)}) while((s32[]{:T(128)}, bf16[16,10,2048]{2,1,0:T(8,128)(2,1)S(1)}, s32[16,2048]{1,0:T(8,128)S(1)}, bf16[10,2048]{1,0:T(8,128)(2,1)S(1)}, s32[]{:T(128)}) %tuple.68), condition=%wide.region_2.3_spmd, body=%wide.region_1.2_spmd.sunk | while | flops 88100864 | bytes 155717 | solution.py:61
  79.9 6.3 %all-to-all-start.1 = ((bf16[10,128,256]{2,0,1:T(8,128)(2,1)}), bf16[10,128,256]{2,0,1:T(8,128)(2,1)S(1)}, u32[]{:S(2)}, u32[]{:S(2)}) async-start(bf16[10,128,256]{2,0,1:T(8,128)(2,1)} %copy.55), calls=%async_computation.1 | async-start | bytes 2097152 | tf_op jit(solution)/shard_map/all_to_all | solution.py:126
  90.1 4.0 %collective-permute-start.4 = (f32[1,128]{1,0:T(1,128)S(1)}, f32[1,128]{1,0:T(1,128)S(1)}, u32[]{:S(2)}, u32[]{:S(2)}) collective-permute-start(f32[1,128]{1,0:T(1,128)S(1)} %get-tuple-element.123), channel_id=1, source_target_pairs={{0,8},{8,16},{16,24},{24,32},{32,40},{40,48},{48,56},{56,64},{64,7... | collective-permute-start | bytes 1544 | tf_op jit(solution)/shard_map/ppermute | solution.py:26
  104.1 11.6 %all-to-all-done.1 = bf16[10,128,256]{2,0,1:T(8,128)(2,1)S(1)} async-done(((bf16[10,128,256]{2,0,1:T(8,128)(2,1)}), bf16[10,128,256]{2,0,1:T(8,128)(2,1)S(1)}, u32[]{:S(2)}, u32[]{:S(2)}) %all-to-all-start.1) | async-done | bytes 655392 | tf_op jit(solution)/shard_map/all_to_all | solution.py:126
  130.8 5.7 %fusion.12 = f32[256,128]{1,0:T(8,128)S(1)} fusion(bf16[10,256,64]{2,0,1:T(8,128)(2,1)} %copy.58, bf16[64,256,128]{2,1,0:T(8,128)(2,1)} %bitcast.96, f32[256,128]{1,0:T(8,128)S(1)} %convert_reduce_fusion, s32[256,128]{1,0:T(8,128)} %bitcast.113), kind=kOutput, calls=%fused_computation.20 | convolution fusion | flops 43220992 | bytes 4915200 | tf_op jit(solution)/shard_map/erb,brj->erj/dot_general | solution.py:134
  146.5 3.8 %collective-permute-done.13 = f32[258,1]{1,0:T(8,128)S(1)} collective-permute-done((f32[258,1]{1,0:T(8,128)S(1)}, f32[258,1]{1,0:T(8,128)S(1)}, u32[]{:S(2)}, u32[]{:S(2)}) %collective-permute-start.13) | collective-permute-done | bytes 1064 | tf_op jit(solution)/shard_map/ppermute | solution.py:29
  163.7 4.1 %collective-permute-done.17 = f32[258,1]{1,0:T(8,128)S(1)} collective-permute-done((f32[258,1]{1,0:T(8,128)S(1)}, f32[258,1]{1,0:T(8,128)S(1)}, u32[]{:S(2)}, u32[]{:S(2)}) %collective-permute-start.17) | collective-permute-done | bytes 1064 | tf_op jit(solution)/shard_map/ppermute | solution.py:29
  168.2 5.2 %collective-permute-start.18 = (f32[1,128]{1,0:T(1,128)S(1)}, f32[1,128]{1,0:T(1,128)S(1)}, u32[]{:S(2)}, u32[]{:S(2)}) collective-permute-start(f32[1,128]{1,0:T(1,128)S(1)} %get-tuple-element.117), channel_id=1, source_target_pairs={{0,8},{8,16},{16,24},{24,32},{32,40},{40,48},{48,56},{56,64},{64,7... | collective-permute-start | bytes 1544 | tf_op jit(solution)/shard_map/ppermute | solution.py:26
  188.4 4.9 %fusion.13 = f32[3,256,64]{2,0,1:T(4,128)S(1)} fusion(bf16[64,256,128]{2,1,0:T(8,128)(2,1)} %bitcast.97, bf16[3,256,128]{2,1,0:T(8,128)(2,1)S(1)} %fusion.20), kind=kOutput, calls=%fused_computation.22 | convolution fusion | flops 12582912 | bytes 4587520 | tf_op jit(solution)/shard_map/brj,qrj->qrb/dot_general | solution.py:154
  194.5 15.4 %collective-permute-start.22 = (f32[3,128,256]{2,1,0:T(8,128)S(1)}, f32[3,128,256]{2,1,0:T(8,128)S(1)}, u32[]{:S(2)}, u32[]{:S(2)}) collective-permute-start(f32[3,128,256]{2,1,0:T(8,128)S(1)} %reshape.36), channel_id=1, source_target_pairs={{128,0},{129,1},{130,2},{131,3},{132,4},{133,5},{134,6},{135,7},{1... | collective-permute-start | bytes 1179656 | tf_op jit(solution)/shard_map/ppermute | solution.py:18
  212.0 12.6 %all-to-all-start.2 = ((f32[3,128,256]{2,0,1:T(4,128)}), f32[3,128,256]{2,0,1:T(4,128)S(1)}, u32[]{:S(2)}, u32[]{:S(2)}) async-start(f32[3,128,256]{2,0,1:T(4,128)} %copy.64), calls=%async_computation.2 | async-start | bytes 1048576 | tf_op jit(solution)/shard_map/all_to_all | solution.py:166
  224.6 19.3 %all-to-all-done.2 = f32[3,128,256]{2,0,1:T(4,128)S(1)} async-done(((f32[3,128,256]{2,0,1:T(4,128)}), f32[3,128,256]{2,0,1:T(4,128)S(1)}, u32[]{:S(2)}, u32[]{:S(2)}) %all-to-all-start.2) | async-done | bytes 393248 | tf_op jit(solution)/shard_map/all_to_all | solution.py:166
  244.1 86.7 %while.22 = (s32[]{:T(128)}, f32[3,2048]{1,0:T(4,128)S(1)}, f32[16,3,2048]{2,0,1:T(8,128)S(1)}, s32[16,2048]{1,0:T(8,128)S(1)}, s32[]{:T(128)}, /*index=5*/s32[]{:T(128)}) while((s32[]{:T(128)}, f32[3,2048]{1,0:T(4,128)S(1)}, f32[16,3,2048]{2,0,1:T(8,128)S(1)}, s32[16,2048]{1,0:T(8,128)S(1)}, s32[]{:T(128)}, ...), condition=%wide.region_6.7_spmd.clone, body=%wide.region_5.6_spmd.clone.sunk | while | flops 155201536 | bytes 147543 | solution.py:83
  244.1 5.4 %fusion.99 = f32[3,2048]{1,0:T(4,128)S(1)} fusion(s32[2048]{0:T(1024)S(1)} %bitcast.106, f32[1,3,2048]{2,0,1:T(1,128)S(1)} %constant_dynamic-slice_fusion.8, f32[3,2048]{1,0:T(4,128)S(1)} %get-tuple-element.197, pred[]{:T(512)S(6)} %compare.3), kind=kOutput, calls=%fused_computation.10.clone.1 | convolution fusion | flops 155201536 | bytes 81921 | tf_op jit(solution)/shard_map/while/body/eval_jaxpr/dot_general | solution.py:74
  249.6 5.4 %fusion.99 = f32[3,2048]{1,0:T(4,128)S(1)} fusion(s32[2048]{0:T(1024)S(1)} %bitcast.106, f32[1,3,2048]{2,0,1:T(1,128)S(1)} %constant_dynamic-slice_fusion.8, f32[3,2048]{1,0:T(4,128)S(1)} %get-tuple-element.197, pred[]{:T(512)S(6)} %compare.3), kind=kOutput, calls=%fused_computation.10.clone.1 | convolution fusion | flops 155201536 | bytes 81921 | tf_op jit(solution)/shard_map/while/body/eval_jaxpr/dot_general | solution.py:74
  255.0 5.4 %fusion.99 = f32[3,2048]{1,0:T(4,128)S(1)} fusion(s32[2048]{0:T(1024)S(1)} %bitcast.106, f32[1,3,2048]{2,0,1:T(1,128)S(1)} %constant_dynamic-slice_fusion.8, f32[3,2048]{1,0:T(4,128)S(1)} %get-tuple-element.197, pred[]{:T(512)S(6)} %compare.3), kind=kOutput, calls=%fused_computation.10.clone.1 | convolution fusion | flops 155201536 | bytes 81921 | tf_op jit(solution)/shard_map/while/body/eval_jaxpr/dot_general | solution.py:74
  260.4 5.4 %fusion.99 = f32[3,2048]{1,0:T(4,128)S(1)} fusion(s32[2048]{0:T(1024)S(1)} %bitcast.106, f32[1,3,2048]{2,0,1:T(1,128)S(1)} %constant_dynamic-slice_fusion.8, f32[3,2048]{1,0:T(4,128)S(1)} %get-tuple-element.197, pred[]{:T(512)S(6)} %compare.3), kind=kOutput, calls=%fused_computation.10.clone.1 | convolution fusion | flops 155201536 | bytes 81921 | tf_op jit(solution)/shard_map/while/body/eval_jaxpr/dot_general | solution.py:74
  265.8 5.4 %fusion.99 = f32[3,2048]{1,0:T(4,128)S(1)} fusion(s32[2048]{0:T(1024)S(1)} %bitcast.106, f32[1,3,2048]{2,0,1:T(1,128)S(1)} %constant_dynamic-slice_fusion.8, f32[3,2048]{1,0:T(4,128)S(1)} %get-tuple-element.197, pred[]{:T(512)S(6)} %compare.3), kind=kOutput, calls=%fused_computation.10.clone.1 | convolution fusion | flops 155201536 | bytes 81921 | tf_op jit(solution)/shard_map/while/body/eval_jaxpr/dot_general | solution.py:74
  271.2 5.4 %fusion.99 = f32[3,2048]{1,0:T(4,128)S(1)} fusion(s32[2048]{0:T(1024)S(1)} %bitcast.106, f32[1,3,2048]{2,0,1:T(1,128)S(1)} %constant_dynamic-slice_fusion.8, f32[3,2048]{1,0:T(4,128)S(1)} %get-tuple-element.197, pred[]{:T(512)S(6)} %compare.3), kind=kOutput, calls=%fused_computation.10.clone.1 | convolution fusion | flops 155201536 | bytes 81921 | tf_op jit(solution)/shard_map/while/body/eval_jaxpr/dot_general | solution.py:74
  276.7 5.4 %fusion.99 = f32[3,2048]{1,0:T(4,128)S(1)} fusion(s32[2048]{0:T(1024)S(1)} %bitcast.106, f32[1,3,2048]{2,0,1:T(1,128)S(1)} %constant_dynamic-slice_fusion.8, f32[3,2048]{1,0:T(4,128)S(1)} %get-tuple-element.197, pred[]{:T(512)S(6)} %compare.3), kind=kOutput, calls=%fused_computation.10.clone.1 | convolution fusion | flops 155201536 | bytes 81921 | tf_op jit(solution)/shard_map/while/body/eval_jaxpr/dot_general | solution.py:74
  282.1 5.4 %fusion.99 = f32[3,2048]{1,0:T(4,128)S(1)} fusion(s32[2048]{0:T(1024)S(1)} %bitcast.106, f32[1,3,2048]{2,0,1:T(1,128)S(1)} %constant_dynamic-slice_fusion.8, f32[3,2048]{1,0:T(4,128)S(1)} %get-tuple-element.197, pred[]{:T(512)S(6)} %compare.3), kind=kOutput, calls=%fused_computation.10.clone.1 | convolution fusion | flops 155201536 | bytes 81921 | tf_op jit(solution)/shard_map/while/body/eval_jaxpr/dot_general | solution.py:74
  287.5 5.4 %fusion.99 = f32[3,2048]{1,0:T(4,128)S(1)} fusion(s32[2048]{0:T(1024)S(1)} %bitcast.106, f32[1,3,2048]{2,0,1:T(1,128)S(1)} %constant_dynamic-slice_fusion.8, f32[3,2048]{1,0:T(4,128)S(1)} %get-tuple-element.197, pred[]{:T(512)S(6)} %compare.3), kind=kOutput, calls=%fused_computation.10.clone.1 | convolution fusion | flops 155201536 | bytes 81921 | tf_op jit(solution)/shard_map/while/body/eval_jaxpr/dot_general | solution.py:74
  292.9 5.4 %fusion.99 = f32[3,2048]{1,0:T(4,128)S(1)} fusion(s32[2048]{0:T(1024)S(1)} %bitcast.106, f32[1,3,2048]{2,0,1:T(1,128)S(1)} %constant_dynamic-slice_fusion.8, f32[3,2048]{1,0:T(4,128)S(1)} %get-tuple-element.197, pred[]{:T(512)S(6)} %compare.3), kind=kOutput, calls=%fused_computation.10.clone.1 | convolution fusion | flops 155201536 | bytes 81921 | tf_op jit(solution)/shard_map/while/body/eval_jaxpr/dot_general | solution.py:74
  298.3 5.4 %fusion.99 = f32[3,2048]{1,0:T(4,128)S(1)} fusion(s32[2048]{0:T(1024)S(1)} %bitcast.106, f32[1,3,2048]{2,0,1:T(1,128)S(1)} %constant_dynamic-slice_fusion.8, f32[3,2048]{1,0:T(4,128)S(1)} %get-tuple-element.197, pred[]{:T(512)S(6)} %compare.3), kind=kOutput, calls=%fused_computation.10.clone.1 | convolution fusion | flops 155201536 | bytes 81921 | tf_op jit(solution)/shard_map/while/body/eval_jaxpr/dot_general | solution.py:74
  303.7 5.4 %fusion.99 = f32[3,2048]{1,0:T(4,128)S(1)} fusion(s32[2048]{0:T(1024)S(1)} %bitcast.106, f32[1,3,2048]{2,0,1:T(1,128)S(1)} %constant_dynamic-slice_fusion.8, f32[3,2048]{1,0:T(4,128)S(1)} %get-tuple-element.197, pred[]{:T(512)S(6)} %compare.3), kind=kOutput, calls=%fused_computation.10.clone.1 | convolution fusion | flops 155201536 | bytes 81921 | tf_op jit(solution)/shard_map/while/body/eval_jaxpr/dot_general | solution.py:74
  309.2 5.4 %fusion.99 = f32[3,2048]{1,0:T(4,128)S(1)} fusion(s32[2048]{0:T(1024)S(1)} %bitcast.106, f32[1,3,2048]{2,0,1:T(1,128)S(1)} %constant_dynamic-slice_fusion.8, f32[3,2048]{1,0:T(4,128)S(1)} %get-tuple-element.197, pred[]{:T(512)S(6)} %compare.3), kind=kOutput, calls=%fused_computation.10.clone.1 | convolution fusion | flops 155201536 | bytes 81921 | tf_op jit(solution)/shard_map/while/body/eval_jaxpr/dot_general | solution.py:74
  314.6 5.4 %fusion.99 = f32[3,2048]{1,0:T(4,128)S(1)} fusion(s32[2048]{0:T(1024)S(1)} %bitcast.106, f32[1,3,2048]{2,0,1:T(1,128)S(1)} %constant_dynamic-slice_fusion.8, f32[3,2048]{1,0:T(4,128)S(1)} %get-tuple-element.197, pred[]{:T(512)S(6)} %compare.3), kind=kOutput, calls=%fused_computation.10.clone.1 | convolution fusion | flops 155201536 | bytes 81921 | tf_op jit(solution)/shard_map/while/body/eval_jaxpr/dot_general | solution.py:74
  320.0 5.4 %fusion.99 = f32[3,2048]{1,0:T(4,128)S(1)} fusion(s32[2048]{0:T(1024)S(1)} %bitcast.106, f32[1,3,2048]{2,0,1:T(1,128)S(1)} %constant_dynamic-slice_fusion.8, f32[3,2048]{1,0:T(4,128)S(1)} %get-tuple-element.197, pred[]{:T(512)S(6)} %compare.3), kind=kOutput, calls=%fused_computation.10.clone.1 | convolution fusion | flops 155201536 | bytes 81921 | tf_op jit(solution)/shard_map/while/body/eval_jaxpr/dot_general | solution.py:74
  325.4 5.4 %fusion.99 = f32[3,2048]{1,0:T(4,128)S(1)} fusion(s32[2048]{0:T(1024)S(1)} %bitcast.106, f32[1,3,2048]{2,0,1:T(1,128)S(1)} %constant_dynamic-slice_fusion.8, f32[3,2048]{1,0:T(4,128)S(1)} %get-tuple-element.197, pred[]{:T(512)S(6)} %compare.3), kind=kOutput, calls=%fused_computation.10.clone.1 | convolution fusion | flops 155201536 | bytes 81921 | tf_op jit(solution)/shard_map/while/body/eval_jaxpr/dot_general | solution.py:74
  (172 shorter events, 122.6 us)
Async XLA Ops:
  3.7 6.1 %collective-permute-start.8 = (s32[128,256]{1,0:T(8,128)S(1)}, s32[128,256]{1,0:T(8,128)S(1)}, u32[]{:S(2)}, u32[]{:S(2)}) collective-permute-start(s32[128,256]{1,0:T(8,128)S(1)} %reshape.34), channel_id=1, source_target_pairs={{128,0},{129,1},{130,2},{131,3},{132,4},{133,5},{134,6},{135,7},{1... | collective-permute-start | bytes 393224 | tf_op jit(solution)/shard_map/ppermute | solution.py:18
  10.6 25.3 %all-to-all-start = ((s32[128,1,256]{2,1,0:T(1,128)}), s32[128,1,256]{2,1,0:T(1,128)S(1)}, u32[]{:S(2)}, u32[]{:S(2)}) async-start(s32[128,1,256]{2,1,0:T(1,128)} %copy.52), calls=%async_computation | async-start | bytes 262144 | tf_op jit(solution)/shard_map/all_to_all | solution.py:120
  77.9 8.4 %copy-start.3 = (f32[1,256,128]{2,1,0:T(8,128)S(1)}, f32[1,256,128]{2,1,0:T(8,128)}, u32[]{:S(2)}) copy-start(f32[1,256,128]{2,1,0:T(8,128)} %param.21) | copy-start | bytes 393220
  77.9 12.2 %copy-start = (f32[1,256,128]{2,1,0:T(8,128)S(1)}, f32[1,256,128]{2,1,0:T(8,128)}, u32[]{:S(2)}) copy-start(f32[1,256,128]{2,1,0:T(8,128)} %param.20) | copy-start | bytes 393220
  79.9 35.7 %all-to-all-start.1 = ((bf16[10,128,256]{2,0,1:T(8,128)(2,1)}), bf16[10,128,256]{2,0,1:T(8,128)(2,1)S(1)}, u32[]{:S(2)}, u32[]{:S(2)}) async-start(bf16[10,128,256]{2,0,1:T(8,128)(2,1)} %copy.55), calls=%async_computation.1 | async-start | bytes 2097152 | tf_op jit(solution)/shard_map/all_to_all | solution.py:126
  86.3 12.4 %collective-permute-start = (f32[2,1,128]{2,1,0:T(1,128)S(1)}, f32[2,1,128]{2,1,0:T(1,128)S(1)}, u32[]{:S(2)}, u32[]{:S(2)}) collective-permute-start(f32[2,1,128]{2,1,0:T(1,128)S(1)} %get-tuple-element.105), channel_id=1, source_target_pairs={{0,8},{8,16},{16,24},{24,32},{32,40},{40,48},{48,56},{56,64},{64,7... | collective-permute-start | bytes 3080 | tf_op jit(solution)/shard_map/ppermute | solution.py:26
  88.8 10.0 %collective-permute-start.1 = (f32[2,1,128]{2,1,0:T(1,128)S(1)}, f32[2,1,128]{2,1,0:T(1,128)S(1)}, u32[]{:S(2)}, u32[]{:S(2)}) collective-permute-start(f32[2,1,128]{2,1,0:T(1,128)S(1)} %get-tuple-element.106), channel_id=1, source_target_pairs={{8,0},{16,8},{24,16},{32,24},{40,32},{48,40},{56,48},{64,56},{72,6... | collective-permute-start | bytes 3080 | tf_op jit(solution)/shard_map/ppermute | solution.py:29
  90.1 8.1 %collective-permute-start.4 = (f32[1,128]{1,0:T(1,128)S(1)}, f32[1,128]{1,0:T(1,128)S(1)}, u32[]{:S(2)}, u32[]{:S(2)}) collective-permute-start(f32[1,128]{1,0:T(1,128)S(1)} %get-tuple-element.123), channel_id=1, source_target_pairs={{0,8},{8,16},{16,24},{24,32},{32,40},{40,48},{48,56},{56,64},{64,7... | collective-permute-start | bytes 1544 | tf_op jit(solution)/shard_map/ppermute | solution.py:26
  94.1 4.6 %collective-permute-start.5 = (f32[1,128]{1,0:T(1,128)S(1)}, f32[1,128]{1,0:T(1,128)S(1)}, u32[]{:S(2)}, u32[]{:S(2)}) collective-permute-start(f32[1,128]{1,0:T(1,128)S(1)} %get-tuple-element.124), channel_id=1, source_target_pairs={{8,0},{16,8},{24,16},{32,24},{40,32},{48,40},{56,48},{64,56},{72,6... | collective-permute-start | bytes 1544 | tf_op jit(solution)/shard_map/ppermute | solution.py:29
  99.7 22.0 %collective-permute-start.2 = (f32[2,258,1]{2,1,0:T(8,128)}, f32[2,258,1]{2,1,0:T(8,128)S(1)}, u32[]{:S(2)}, u32[]{:S(2)}) collective-permute-start(f32[2,258,1]{2,1,0:T(8,128)} %get-tuple-element.103), channel_id=1, source_target_pairs={{0,1},{1,2},{2,3},{3,4},{4,5},{5,6},{6,7},{8,9},{9,10},{10,11},{11... | collective-permute-start | bytes 6200 | tf_op jit(solution)/shard_map/ppermute | solution.py:26
  102.8 18.9 %collective-permute-start.3 = (f32[2,258,1]{2,1,0:T(8,128)S(1)}, f32[2,258,1]{2,1,0:T(8,128)S(1)}, u32[]{:S(2)}, u32[]{:S(2)}) collective-permute-start(f32[2,258,1]{2,1,0:T(8,128)S(1)} %get-tuple-element.104), channel_id=1, source_target_pairs={{1,0},{2,1},{3,2},{4,3},{5,4},{6,5},{7,6},{9,8},{10,9},{11,10},{12... | collective-permute-start | bytes 6200 | tf_op jit(solution)/shard_map/ppermute | solution.py:29
  115.9 10.2 %collective-permute-start.9 = (bf16[10,128,256]{2,1,0:T(8,128)(2,1)S(1)}, bf16[10,128,256]{2,1,0:T(8,128)(2,1)}, u32[]{:S(2)}, u32[]{:S(2)}) collective-permute-start(bf16[10,128,256]{2,1,0:T(8,128)(2,1)S(1)} %copy.56), channel_id=1, source_target_pairs={{0,128},{1,129},{2,130},{3,131},{4,132},{5,133},{6,134},{7,135},{8... | collective-permute-start | bytes 1966088 | tf_op jit(solution)/shard_map/ppermute | solution.py:18
  117.3 4.8 %collective-permute-start.6 = (f32[258,1]{1,0:T(8,128)S(1)}, f32[258,1]{1,0:T(8,128)S(1)}, u32[]{:S(2)}, u32[]{:S(2)}) collective-permute-start(f32[258,1]{1,0:T(8,128)S(1)} %get-tuple-element.113), channel_id=1, source_target_pairs={{0,1},{1,2},{2,3},{3,4},{4,5},{5,6},{6,7},{8,9},{9,10},{10,11},{11... | collective-permute-start | bytes 3104 | tf_op jit(solution)/shard_map/ppermute | solution.py:26
  120.1 5.8 %collective-permute-start.7 = (f32[258,1]{1,0:T(8,128)S(1)}, f32[258,1]{1,0:T(8,128)S(1)}, u32[]{:S(2)}, u32[]{:S(2)}) collective-permute-start(f32[258,1]{1,0:T(8,128)S(1)} %get-tuple-element.114), channel_id=1, source_target_pairs={{1,0},{2,1},{3,2},{4,3},{5,4},{6,5},{7,6},{9,8},{10,9},{11,10},{12... | collective-permute-start | bytes 3104 | tf_op jit(solution)/shard_map/ppermute | solution.py:29
  130.8 5.7 %copy-start.1 = (s32[1,256,128]{2,1,0:T(8,128)S(1)}, s32[1,256,128]{2,1,0:T(8,128)}, u32[]{:S(2)}) copy-start(s32[1,256,128]{2,1,0:T(8,128)} %param.18) | copy-start | bytes 393220
  136.8 2.6 collective-permute-start.10
  138.1 4.3 %collective-permute-start.11 = (f32[1,128]{1,0:T(1,128)S(1)}, f32[1,128]{1,0:T(1,128)S(1)}, u32[]{:S(2)}, u32[]{:S(2)}) collective-permute-start(f32[1,128]{1,0:T(1,128)S(1)} %get-tuple-element.122), channel_id=1, source_target_pairs={{8,0},{16,8},{24,16},{32,24},{40,32},{48,40},{56,48},{64,56},{72,6... | collective-permute-start | bytes 1544 | tf_op jit(solution)/shard_map/ppermute | solution.py:29
  142.6 3.9 %collective-permute-start.12 = (f32[258,1]{1,0:T(8,128)S(1)}, f32[258,1]{1,0:T(8,128)S(1)}, u32[]{:S(2)}, u32[]{:S(2)}) collective-permute-start(f32[258,1]{1,0:T(8,128)S(1)} %get-tuple-element.111), channel_id=1, source_target_pairs={{0,1},{1,2},{2,3},{3,4},{4,5},{5,6},{6,7},{8,9},{9,10},{10,11},{11... | collective-permute-start | bytes 3104 | tf_op jit(solution)/shard_map/ppermute | solution.py:26
  144.5 5.8 %collective-permute-start.13 = (f32[258,1]{1,0:T(8,128)S(1)}, f32[258,1]{1,0:T(8,128)S(1)}, u32[]{:S(2)}, u32[]{:S(2)}) collective-permute-start(f32[258,1]{1,0:T(8,128)S(1)} %get-tuple-element.112), channel_id=1, source_target_pairs={{1,0},{2,1},{3,2},{4,3},{5,4},{6,5},{7,6},{9,8},{10,9},{11,10},{12... | collective-permute-start | bytes 3104 | tf_op jit(solution)/shard_map/ppermute | solution.py:29
  150.4 37.8 %copy-start.2 = (f32[1,256,128]{2,1,0:T(8,128)S(1)}, f32[1,256,128]{2,1,0:T(8,128)}, u32[]{:S(2)}) copy-start(f32[1,256,128]{2,1,0:T(8,128)} %param.19) | copy-start | bytes 393220
  150.7 3.9 %collective-permute-start.14 = (f32[1,128]{1,0:T(1,128)S(1)}, f32[1,128]{1,0:T(1,128)S(1)}, u32[]{:S(2)}, u32[]{:S(2)}) collective-permute-start(f32[1,128]{1,0:T(1,128)S(1)} %get-tuple-element.119), channel_id=1, source_target_pairs={{0,8},{8,16},{16,24},{24,32},{32,40},{40,48},{48,56},{56,64},{64,7... | collective-permute-start | bytes 1544 | tf_op jit(solution)/shard_map/ppermute | solution.py:26
  153.2 4.6 %collective-permute-start.15 = (f32[1,128]{1,0:T(1,128)S(1)}, f32[1,128]{1,0:T(1,128)S(1)}, u32[]{:S(2)}, u32[]{:S(2)}) collective-permute-start(f32[1,128]{1,0:T(1,128)S(1)} %get-tuple-element.120), channel_id=1, source_target_pairs={{8,0},{16,8},{24,16},{32,24},{40,32},{48,40},{56,48},{64,56},{72,6... | collective-permute-start | bytes 1544 | tf_op jit(solution)/shard_map/ppermute | solution.py:29
  158.0 5.7 %collective-permute-start.16 = (f32[258,1]{1,0:T(8,128)S(1)}, f32[258,1]{1,0:T(8,128)S(1)}, u32[]{:S(2)}, u32[]{:S(2)}) collective-permute-start(f32[258,1]{1,0:T(8,128)S(1)} %get-tuple-element.109), channel_id=1, source_target_pairs={{0,1},{1,2},{2,3},{3,4},{4,5},{5,6},{6,7},{8,9},{9,10},{10,11},{11... | collective-permute-start | bytes 3104 | tf_op jit(solution)/shard_map/ppermute | solution.py:26
  161.7 6.1 %collective-permute-start.17 = (f32[258,1]{1,0:T(8,128)S(1)}, f32[258,1]{1,0:T(8,128)S(1)}, u32[]{:S(2)}, u32[]{:S(2)}) collective-permute-start(f32[258,1]{1,0:T(8,128)S(1)} %get-tuple-element.110), channel_id=1, source_target_pairs={{1,0},{2,1},{3,2},{4,3},{5,4},{6,5},{7,6},{9,8},{10,9},{11,10},{12... | collective-permute-start | bytes 3104 | tf_op jit(solution)/shard_map/ppermute | solution.py:29
  168.2 6.5 %collective-permute-start.18 = (f32[1,128]{1,0:T(1,128)S(1)}, f32[1,128]{1,0:T(1,128)S(1)}, u32[]{:S(2)}, u32[]{:S(2)}) collective-permute-start(f32[1,128]{1,0:T(1,128)S(1)} %get-tuple-element.117), channel_id=1, source_target_pairs={{0,8},{8,16},{16,24},{24,32},{32,40},{40,48},{48,56},{56,64},{64,7... | collective-permute-start | bytes 1544 | tf_op jit(solution)/shard_map/ppermute | solution.py:26
  173.4 4.5 %collective-permute-start.19 = (f32[1,128]{1,0:T(1,128)S(1)}, f32[1,128]{1,0:T(1,128)S(1)}, u32[]{:S(2)}, u32[]{:S(2)}) collective-permute-start(f32[1,128]{1,0:T(1,128)S(1)} %get-tuple-element.118), channel_id=1, source_target_pairs={{8,0},{16,8},{24,16},{32,24},{40,32},{48,40},{56,48},{64,56},{72,6... | collective-permute-start | bytes 1544 | tf_op jit(solution)/shard_map/ppermute | solution.py:29
  178.0 5.4 %collective-permute-start.20 = (f32[258,1]{1,0:T(8,128)S(1)}, f32[258,1]{1,0:T(8,128)S(1)}, u32[]{:S(2)}, u32[]{:S(2)}) collective-permute-start(f32[258,1]{1,0:T(8,128)S(1)} %get-tuple-element.107), channel_id=1, source_target_pairs={{0,1},{1,2},{2,3},{3,4},{4,5},{5,6},{6,7},{8,9},{9,10},{10,11},{11... | collective-permute-start | bytes 3104 | tf_op jit(solution)/shard_map/ppermute | solution.py:26
  181.5 5.8 %collective-permute-start.21 = (f32[258,1]{1,0:T(8,128)S(1)}, f32[258,1]{1,0:T(8,128)S(1)}, u32[]{:S(2)}, u32[]{:S(2)}) collective-permute-start(f32[258,1]{1,0:T(8,128)S(1)} %get-tuple-element.108), channel_id=1, source_target_pairs={{1,0},{2,1},{3,2},{4,3},{5,4},{6,5},{7,6},{9,8},{10,9},{11,10},{12... | collective-permute-start | bytes 3104 | tf_op jit(solution)/shard_map/ppermute | solution.py:29
  194.5 16.5 %collective-permute-start.22 = (f32[3,128,256]{2,1,0:T(8,128)S(1)}, f32[3,128,256]{2,1,0:T(8,128)S(1)}, u32[]{:S(2)}, u32[]{:S(2)}) collective-permute-start(f32[3,128,256]{2,1,0:T(8,128)S(1)} %reshape.36), channel_id=1, source_target_pairs={{128,0},{129,1},{130,2},{131,3},{132,4},{133,5},{134,6},{135,7},{1... | collective-permute-start | bytes 1179656 | tf_op jit(solution)/shard_map/ppermute | solution.py:18
  212.0 31.9 %all-to-all-start.2 = ((f32[3,128,256]{2,0,1:T(4,128)}), f32[3,128,256]{2,0,1:T(4,128)S(1)}, u32[]{:S(2)}, u32[]{:S(2)}) async-start(f32[3,128,256]{2,0,1:T(4,128)} %copy.64), calls=%async_computation.2 | async-start | bytes 1048576 | tf_op jit(solution)/shard_map/all_to_all | solution.py:166
where the time goes:
time: 333 us; the launch traced here: 331 us
  matrix products  140 us (42%)
  starting transfers between devices  98.2 us (29%)
  waiting for transfers between devices  70.1 us (21%)
  local copies, waits for them, and re-layouts  13.3 us (4%)
  other arithmetic  8.27 us (2%)
    dot_general x16, matrix products, add_one_block(): jnp.dot(value_block, onehot.astype(jnp.float32), precision=FULL_PRECISION...  85.7 us
    dot_general x16, matrix products, pick_one_block(): jnp.dot(table, onehot.astype(jnp.bfloat16), preferred_element_type=jnp.fl...  41.4 us
    ppermute x10, starting transfers between devices, padded_2(): lax.ppermute(lax.slice_in_dim(block, block.shape[dim] - width, None, axis...  30.6 us
    ppermute x10, waiting for transfers between devices, padded_2(): lax.ppermute(lax.slice_in_dim(block, 0, width, axis=dim), axis, backward)  25.5 us
    ppermute x3, starting transfers between devices, shifted(): lax.ppermute(value, axis, [(source, source + steps) for source in range(i...  21.8 us
    all_to_all x1, waiting for transfers between devices, per_device(): lax.all_to_all(outgoing, ('gx', 'gy'), split_axis=1, concat_axis=1, tiled...  19.3 us
    all_to_all x1, starting transfers between devices, per_device(): lax.all_to_all(wanted, ('gx', 'gy'), split_axis=0, concat_axis=0, tiled=T...  13.8 us
    ppermute x10, starting transfers between devices, padded_2(): lax.ppermute(lax.slice_in_dim(block, 0, width, axis=dim), axis, backward)  13.1 us
  transfers between devices with their start and end apart: 26, of which 17 were waited for; matrix products, arithmetic and copies ran while one was open for 2% of the time, Pallas kernels for 0%

commit v1 on v0

v1 whole, which is shorter than its diff:
```python
import jax
import jax.numpy as jnp
from jax import lax
from jax.experimental import pallas as pl
from jax.experimental.pallas import tpu as pltpu
from jax.sharding import PartitionSpec as P

STEPS = 4
SMB_RATE = 0.5
LOW = 256
PLANES = ("gx", "gy")
F32 = jnp.float32
BF16 = jnp.bfloat16


def neighbours(axis, value, low_edge, high_edge):
    count = lax.axis_size(axis)
    forward = [(i, i + 1) for i in range(count - 1)]
    backward = [(i + 1, i) for i in range(count - 1)]
    from_low = lax.ppermute(high_edge, axis, forward)
    from_high = lax.ppermute(low_edge, axis, backward)
    return from_low, from_high


def padded_halo(block, width):
    count, rows, cols = block.shape
    turn = lambda part: jnp.transpose(part, (0, 2, 1))
    left, right = neighbours(
        "gy", block, turn(block[:, :, :width]), turn(block[:, :, cols - width :])
    )
    block = jnp.concatenate([turn(left), block, turn(right)], axis=2)
    above, below = neighbours("gx", block, block[:, :width], block[:, rows - width :])
    return jnp.concatenate([above, block, below], axis=1)


def pick_kernel(table_ref, index_ref, out_ref):
    sources = index_ref.shape[0]
    classes = out_ref.shape[1]
    high_count = table_ref.shape[0] // 16
    table = table_ref[...]
    low_iota = lax.broadcasted_iota(jnp.int32, (LOW, 128), 0)
    for s in range(0, sources, 2):
        hot = []
        high = []
        for d in range(2):
            row = index_ref[s + d : s + d + 1, :]
            hot.append((low_iota == (row & (LOW - 1))).astype(F32).astype(BF16))
            high.append(jnp.broadcast_to(row // LOW, (16, 128)))
        found = jnp.dot(
            table, jnp.concatenate(hot, axis=1), preferred_element_type=F32
        )
        for d in range(2):
            part = found[:, 128 * d : 128 * d + 128]
            total = part[:16]
            for h in range(1, high_count):
                total = jnp.where(high[d] == h, part[16 * h : 16 * h + 16], total)
            out_ref[s + d] = total[:classes].astype(BF16)


def pick(table, asked, classes):
    sources = asked.shape[0]
    step = 16
    return pl.pallas_call(
        pick_kernel,
        grid=(sources // step,),
        in_specs=[
            pl.BlockSpec(table.shape, lambda i: (0, 0)),
            pl.BlockSpec((step, 128), lambda i: (i, 0)),
        ],
        out_specs=pl.BlockSpec((step, classes, 128), lambda i: (i, 0, 0)),
        out_shape=jax.ShapeDtypeStruct((sources, classes, 128), BF16),
        name="pick",
    )(table, asked)


def scatter_kernel(index_ref, value_ref, out_ref):
    sources = index_ref.shape[0]
    high_count = out_ref.shape[0] // 3
    low_iota = lax.broadcasted_iota(jnp.int32, (LOW, 128), 0)
    high_iota = lax.broadcasted_iota(jnp.int32, (high_count, 128), 0)
    hot = []
    spread = []
    for s in range(sources):
        row = index_ref[s : s + 1, :]
        hot.append((low_iota == (row & (LOW - 1))).astype(F32).astype(BF16))
        mine = high_iota == row // LOW
        values = value_ref[s]
        first = values.astype(BF16).astype(F32)
        rest = values - first
        rows = []
        for part in (first, rest):
            for q in range(3):
                rows.append(jnp.where(mine, part[q : q + 1], 0.0))
        spread.append(jnp.concatenate(rows, axis=0).astype(BF16))
    sums = lax.dot_general(
        jnp.concatenate(spread, axis=1),
        jnp.concatenate(hot, axis=1),
        (((1,), (1,)), ((), ())),
        preferred_element_type=F32,
    )
    sums = sums[: 3 * high_count] + sums[3 * high_count :]

    @pl.when(pl.program_id(0) == 0)
    def _():
        out_ref[...] = sums

    @pl.when(pl.program_id(0) > 0)
    def _():
        out_ref[...] += sums


def scatter(asked, values, high_count):
    sources = asked.shape[0]
    step = 16
    return pl.pallas_call(
        scatter_kernel,
        grid=(sources // step,),
        in_specs=[
            pl.BlockSpec((step, 128), lambda i: (i, 0)),
            pl.BlockSpec((step, 3, 128), lambda i: (i, 0, 0)),
        ],
        out_specs=pl.BlockSpec((3 * high_count, LOW), lambda i: (0, 0)),
        out_shape=jax.ShapeDtypeStruct((3 * high_count, LOW), F32),
        name="scatter",
    )(asked, values)


def relax(thick, bed, diff, source, inside):
    surface = bed + thick
    centre = surface[1:-1, 1:-1]
    centre_diff = diff[1:-1, 1:-1]
    change = jnp.zeros_like(centre)
    for near, near_diff in (
        (surface[2:, 1:-1], diff[2:, 1:-1]),
        (surface[:-2, 1:-1], diff[:-2, 1:-1]),
        (surface[1:-1, 2:], diff[1:-1, 2:]),
        (surface[1:-1, :-2], diff[1:-1, :-2]),
    ):
        change = change + 0.5 * (centre_diff + near_diff) * (near - centre)
    return jnp.maximum(thick[1:-1, 1:-1] + change + SMB_RATE * source, 0.0) * inside


def per_device(
    fluxes, weights, land_rows, owners, elev_class, ice_mask, bed, thickness, diffusivity
):
    groups = lax.axis_size("gx") * lax.axis_size("gy")
    is_ice = lax.axis_index("grp") == 1
    block_weights = weights[0]
    local_rows = land_rows[0]
    row_count, width = local_rows.shape
    col_count = block_weights.shape[2]
    classes, cells = fluxes.shape[1:]
    high_count = cells // LOW

    table = jnp.pad(fluxes[0].astype(BF16), ((0, 16 - classes), (0, 0)))
    table = jnp.transpose(table.reshape(16, high_count, LOW), (1, 0, 2)).reshape(-1, LOW)
    table = jnp.where(is_ice, lax.ppermute(table, "grp", [(0, 1)]), table)

    owner_row = owners.reshape(1, row_count)
    named = lax.broadcasted_iota(jnp.int32, (groups, row_count), 0) == owner_row
    earlier = lax.broadcasted_iota(jnp.int32, (row_count, row_count), 0) < (
        lax.broadcasted_iota(jnp.int32, (row_count, row_count), 1)
    )
    rank = jnp.dot(named.astype(BF16), earlier.astype(BF16), preferred_element_type=F32)
    place = jnp.stack([named & (rank == k) for k in range(4)]).astype(BF16)
    digits = jnp.concatenate([local_rows // 8, local_rows % 8], axis=1).astype(BF16)
    wanted = jnp.einsum("kor,rb->kob", place, digits, preferred_element_type=F32)
    wanted = (8.0 * wanted[..., :width] + wanted[..., width:]).astype(jnp.int32)
    wanted = [jnp.concatenate([wanted[k], wanted[k + 1]], axis=1) for k in (0, 2)]
    request = jnp.where(is_ice, wanted[0], lax.ppermute(wanted[1], "grp", [(1, 0)]))
    asked = lax.all_to_all(request, PLANES, split_axis=0, concat_axis=0, tiled=True)

    answer = pick(table, asked, classes)
    answer = answer.reshape(groups, classes // 2, 2, 128)
    answer = lax.all_to_all(answer, PLANES, split_axis=0, concat_axis=0, tiled=True)
    answer = answer.reshape(groups, classes, 2, width)
    other = lax.ppermute(answer, "grp", [(0, 1)])
    picked = sum(
        jnp.einsum(
            "or,oeb->reb",
            place[k],
            (answer, other)[k // 2][:, :, k % 2],
            preferred_element_type=F32,
        )
        for k in range(4)
    ).astype(BF16)

    weight_total = jnp.sum(block_weights, axis=0, dtype=F32)
    remapped = jnp.einsum(
        "reb,brj->erj", picked, block_weights, preferred_element_type=F32
    )
    keep_mask = ice_mask[0].astype(F32)
    level = jnp.arange(classes, dtype=jnp.int32)[:, None, None]
    source = keep_mask * (
        jnp.sum(jnp.where(elev_class[0][None] == level, remapped, 0.0), axis=0) / weight_total
    )

    fixed = padded_halo(jnp.stack([bed[0], diffusivity[0], thickness[0]]), STEPS)
    source_pad = padded_halo(source[None], STEPS - 1)[0]
    row_at = lax.axis_index("gx") * row_count - STEPS + lax.broadcasted_iota(
        jnp.int32, fixed.shape[1:], 0
    )
    col_at = lax.axis_index("gy") * col_count - STEPS + lax.broadcasted_iota(
        jnp.int32, fixed.shape[1:], 1
    )
    inside = (
        (row_at >= 0)
        & (row_at < row_count * lax.axis_size("gx"))
        & (col_at >= 0)
        & (col_at < col_count * lax.axis_size("gy"))
    ).astype(F32)
    bed_pad, diff_pad, thick = fixed[0], fixed[1], fixed[2]
    for step in range(STEPS):
        trim = lambda a, n: a[n : a.shape[0] - n, n : a.shape[1] - n] if n else a
        thick = relax(
            thick,
            trim(bed_pad, step),
            trim(diff_pad, step),
            trim(source_pad, step),
            trim(inside, step + 1),
        )

    surface = bed[0] + thick
    fraction = keep_mask * jnp.minimum(thick, 1.0)
    fields = (jnp.stack([surface, fraction, jnp.ones_like(surface)]) / weight_total).astype(BF16)
    partial = jnp.einsum("brj,qrj->qrb", block_weights, fields, preferred_element_type=F32)
    outgoing = jnp.einsum(
        "kor,qrb->koqb",
        place.astype(F32),
        partial,
        precision=lax.Precision.HIGHEST,
        preferred_element_type=F32,
    )
    outgoing = [jnp.concatenate([outgoing[k], outgoing[k + 1]], axis=2) for k in (0, 2)]
    sent = jnp.where(is_ice, outgoing[0], lax.ppermute(outgoing[1], "grp", [(1, 0)]))
    arrived = lax.all_to_all(sent, PLANES, split_axis=0, concat_axis=0, tiled=True)
    land_sums = scatter(asked, arrived, high_count)
    land_sums = land_sums + lax.ppermute(land_sums, "grp", [(1, 0)])
    land_sums = land_sums.reshape(3, cells)
    averaged = land_sums[:2] / jnp.maximum(land_sums[2], 1.0)
    land_fields = jnp.where(is_ice, 0.0, averaged)[None]
    thickness_new = jnp.where(is_ice, thick, 0.0)[None]
    return (land_fields, thickness_new)


def solution(mesh):
    return jax.shard_map(
        per_device,
        mesh=mesh,
        in_specs=(
            P("grp", None, ("gx", "gy")),
            P("grp", None, "gx", "gy"),
            P("grp", "gx", "gy"),
            P("grp", "gx", "gy", None, None),
            P("grp", "gx", "gy"),
            P("grp", "gx", "gy"),
            P("grp", "gx", "gy"),
            P("grp", "gx", "gy"),
            P("grp", "gx", "gy"),
        ),
        out_specs=(P("grp", None, ("gx", "gy")), P("grp", "gx", "gy")),
        check_vma=False,
    )
```

time: 333 us -> 158 us (0.47)
  matrix products: 140 us -> 10.6 us
  starting transfers between devices: 98.2 us -> 55.1 us
  waiting for transfers between devices: 70.1 us -> 30.8 us
  blocking collectives: 0 us -> 28.6 us
  Pallas kernels: 0 us -> 11.5 us
  local copies, waits for them, and re-layouts: 13.3 us -> 8.41 us
    dot_general x34 -> x4, matrix products: 134 us -> 7.04 us  [the longest x1 5.3 us: per_device(): jnp.einsum('reb,brj->erj', picked, block_weights, preferred_element_type=...]
    ppermute x23 -> x13, starting transfers between devices: 65.4 us -> 31.7 us  [the longest x4 10.6 us: neighbours(): from_low = lax.ppermute(high_edge, axis, forward)]
    all_to_all x0 -> x1, blocking collectives: none -> 28.6 us  [per_device(): lax.all_to_all(sent, PLANES, split_axis=0, concat_axis=0, tiled=True)]
    all_to_all x3 -> x2, waiting for transfers between devices: 40.5 us -> 15.4 us  [the longest x1 9.87 us: per_device(): lax.all_to_all(request, PLANES, split_axis=0, concat_axis=0, tiled=True)]
    ppermute x23 -> x13, waiting for transfers between devices: 29.6 us -> 15.4 us  [the longest x4 7.14 us: neighbours(): from_high = lax.ppermute(low_edge, axis, backward)]
    pallas_call x0 -> x2, Pallas kernels: none -> 11.5 us  [the longest x1 5.95 us: scatter(): pl.pallas_call(scatter_kernel, grid=(sources // step,), in_specs=[pl.Bloc...]
    all_to_all x3 -> x2, starting transfers between devices: 32.7 us -> 23.3 us  [the longest x1 17.1 us: per_device(): lax.all_to_all(request, PLANES, split_axis=0, concat_axis=0, tiled=True)]
  transfers between devices with their start and end apart: 26 -> 15, of which waited for: 17 -> 9; matrix products, arithmetic and copies ran while one was open for 2% -> 6% of each run, Pallas kernels for 0% -> 4%
where the time goes in v1:
time: 158 us; the launch traced here: 157 us
  starting transfers between devices  55.1 us (35%)
  waiting for transfers between devices  30.8 us (19%)
  blocking collectives  28.6 us (18%)
  Pallas kernels  11.5 us (7%)
  matrix products  10.6 us (7%)
  other arithmetic  10.3 us (7%)
  local copies, waits for them, and re-layouts  8.41 us (5%)
    all_to_all x1, blocking collectives, per_device(): lax.all_to_all(sent, PLANES, split_axis=0, concat_axis=0, tiled=True)  28.6 us
    all_to_all x1, starting transfers between devices, per_device(): lax.all_to_all(request, PLANES, split_axis=0, concat_axis=0, tiled=True)  17.1 us
    ppermute x4, starting transfers between devices, neighbours(): from_low = lax.ppermute(high_edge, axis, forward)  10.6 us
    all_to_all x1, waiting for transfers between devices, per_device(): lax.all_to_all(request, PLANES, split_axis=0, concat_axis=0, tiled=True)  9.87 us
    ppermute x4, waiting for transfers between devices, neighbours(): from_high = lax.ppermute(low_edge, axis, backward)  7.14 us
    all_to_all x1, starting transfers between devices, per_device(): lax.all_to_all(answer, PLANES, split_axis=0, concat_axis=0, tiled=True)  6.18 us
    pallas_call x1, Pallas kernels, scatter(): pl.pallas_call(scatter_kernel, grid=(sources // step,), in_specs=[pl.Bloc...  5.95 us
    all_to_all x1, waiting for transfers between devices, per_device(): lax.all_to_all(answer, PLANES, split_axis=0, concat_axis=0, tiled=True)  5.56 us
  transfers between devices with their start and end apart: 15, of which 9 were waited for; matrix products, arithmetic and copies ran while one was open for 6% of the time, Pallas kernels for 4%

profile of v1, /device:TPU:1, one launch (start us, length us, event | category | flops | bytes accessed | tf_op | source)
XLA Modules:
  0.0 156.6 jit_solution(16966866856409123908)
XLA Ops:
  0.7 1.1 fusion.78
  1.8 1.1 fusion.79
  3.2 5.1 %collective-permute-start = (s32[128,128]{0,1:T(8,128)S(1)}, s32[128,128]{0,1:T(8,128)S(1)}, u32[]{:S(2)}, u32[]{:S(2)}) collective-permute-start(s32[128,128]{0,1:T(8,128)S(1)} %pad_add_fusion.1), channel_id=1, source_target_pairs={{128,0},{129,1},{130,2},{131,3},{132,4},{133,5},{134,6},{135,7},{1... | collective-permute-start | bytes 196616 | tf_op jit(solution)/shard_map/ppermute | solution.py:170
  9.3 1.3 collective-permute-start.5
  12.7 1.9 %collective-permute-start.1 = (f32[3,4,256]{1,2,0:T(8,128)S(1)}, f32[3,4,256]{1,2,0:T(8,128)S(1)}, u32[]{:S(2)}, u32[]{:S(2)}) collective-permute-start(f32[3,4,256]{1,2,0:T(8,128)S(1)} %get-tuple-element.22), channel_id=1, source_target_pairs={{0,1},{1,2},{2,3},{3,4},{4,5},{5,6},{6,7},{8,9},{9,10},{10,11},{11... | collective-permute-start | bytes 36872 | tf_op jit(solution)/shard_map/ppermute | solution.py:20
  14.5 1.3 collective-permute-start.2
  17.2 17.1 %all-to-all-start = ((s32[128,1,128]{2,1,0:T(1,128)}), s32[128,1,128]{2,1,0:T(1,128)S(1)}, u32[]{:S(2)}, u32[]{:S(2)}) async-start(s32[128,1,128]{2,1,0:T(1,128)} %copy.29), calls=%async_computation | async-start | bytes 131072 | tf_op jit(solution)/shard_map/all_to_all | solution.py:171
  35.0 9.9 %all-to-all-done = s32[128,1,128]{2,1,0:T(1,128)S(1)} async-done(((s32[128,1,128]{2,1,0:T(1,128)}), s32[128,1,128]{2,1,0:T(1,128)S(1)}, u32[]{:S(2)}, u32[]{:S(2)}) %all-to-all-start) | async-done | bytes 65568 | tf_op jit(solution)/shard_map/all_to_all | solution.py:171
  45.5 5.5 %pick.1 = bf16[128,10,128]{2,1,0:T(8,128)(2,1)} custom-call(bf16[128,256]{1,0:T(8,128)(2,1)} %broadcast_select_fusion.table_ref, s32[128,128]{1,0:T(8,128)} %bitcast.170), custom_call_target="tpu_custom_call" | custom-call | tf_op jit(solution)/shard_map/pick/pallas_call | solution.py:63
  51.0 1.1 copy.31
  52.1 1.1 copy.32
  53.2 6.2 %all-to-all-start.1 = ((bf16[128,5,2,128]{3,2,1,0:T(2,128)(2,1)}), bf16[128,5,2,128]{3,2,1,0:T(2,128)(2,1)S(1)}, u32[]{:S(2)}, u32[]{:S(2)}) async-start(bf16[128,5,2,128]{3,2,1,0:T(2,128)(2,1)} %copy.32), calls=%async_computation.1 | async-start | bytes 655360 | tf_op jit(solution)/shard_map/all_to_all | solution.py:175
  59.5 2.4 %collective-permute-start.3 = (f32[3,4,136]{2,1,0:T(4,128)S(1)}, f32[3,4,136]{2,1,0:T(4,128)S(1)}, u32[]{:S(2)}, u32[]{:S(2)}) collective-permute-start(f32[3,4,136]{2,1,0:T(4,128)S(1)} %get-tuple-element.11), channel_id=1, source_target_pairs={{0,8},{8,16},{16,24},{24,32},{32,40},{40,48},{48,56},{56,64},{64,7... | collective-permute-start | bytes 19592 | tf_op jit(solution)/shard_map/ppermute | solution.py:20
  62.0 1.3 collective-permute-start.4
  63.5 3.3 %collective-permute-done.4 = f32[3,4,136]{2,1,0:T(4,128)S(1)} collective-permute-done((f32[3,4,136]{2,1,0:T(4,128)S(1)}, f32[3,4,136]{2,1,0:T(4,128)S(1)}, u32[]{:S(2)}, u32[]{:S(2)}) %collective-permute-start.4) | collective-permute-done | bytes 6560 | tf_op jit(solution)/shard_map/ppermute | solution.py:21
  67.1 5.6 %all-to-all-done.1 = bf16[128,5,2,128]{3,2,1,0:T(2,128)(2,1)S(1)} async-done(((bf16[128,5,2,128]{3,2,1,0:T(2,128)(2,1)}), bf16[128,5,2,128]{3,2,1,0:T(2,128)(2,1)S(1)}, u32[]{:S(2)}, u32[]{:S(2)}) %all-to-all-start.1) | async-done | bytes 327712 | tf_op jit(solution)/shard_map/all_to_all | solution.py:175
  73.4 1.5 collective-permute-start.6
  75.4 4.6 %collective-permute-done.6 = bf16[128,10,2,64]{0,3,2,1:T(8,128)(2,1)S(1)} collective-permute-done((bf16[128,10,2,64]{0,3,2,1:T(8,128)(2,1)S(1)}, bf16[128,10,2,64]{0,3,2,1:T(8,128)(2,1)S(1)}, u32[]{:S(2)}, u32[]{:S(2)}) %collective-permute-start.6) | collective-permute-done | bytes 327712 | tf_op jit(solution)/shard_map/ppermute | solution.py:177
  81.7 5.3 %fusion.4 = f32[256,128]{1,0:T(8,128)S(1)} fusion(bf16[256,10,64]{2,1,0:T(8,128)(2,1)S(1)} %copy.34, bf16[64,256,128]{2,1,0:T(8,128)(2,1)} %bitcast.149, s32[256,128]{1,0:T(8,128)S(1)} %bitcast.189), kind=kOutput, calls=%fused_computation.6 | convolution fusion | flops 42893312 | bytes 4784128 | tf_op jit(solution)/shard_map/reb,brj->erj/dot_general | solution.py:189
  87.2 2.1 %collective-permute-start.7 = (f32[1,3,256]{1,2,0:T(8,128)S(1)}, f32[1,3,256]{1,2,0:T(8,128)S(1)}, u32[]{:S(2)}, u32[]{:S(2)}) collective-permute-start(f32[1,3,256]{1,2,0:T(8,128)S(1)} %get-tuple-element.34), channel_id=1, source_target_pairs={{0,1},{1,2},{2,3},{3,4},{4,5},{5,6},{6,7},{8,9},{9,10},{10,11},{11... | collective-permute-start | bytes 9224 | tf_op jit(solution)/shard_map/ppermute | solution.py:20
  89.3 1.3 collective-permute-start.8
  90.7 1.3 collective-permute-done.7
  92.0 3.8 %collective-permute-done.8 = f32[1,3,256]{1,2,0:T(8,128)S(1)} collective-permute-done((f32[1,3,256]{1,2,0:T(8,128)S(1)}, f32[1,3,256]{1,2,0:T(8,128)S(1)}, u32[]{:S(2)}, u32[]{:S(2)}) %collective-permute-start.8) | collective-permute-done | bytes 3104 | tf_op jit(solution)/shard_map/ppermute | solution.py:21
  95.9 1.3 collective-permute-start.10
  97.2 4.2 %collective-permute-start.9 = (f32[1,3,134]{2,1,0:T(4,128)S(1)}, f32[1,3,134]{2,1,0:T(4,128)S(1)}, u32[]{:S(2)}, u32[]{:S(2)}) collective-permute-start(f32[1,3,134]{2,1,0:T(4,128)S(1)} %get-tuple-element.20), channel_id=1, source_target_pairs={{0,8},{8,16},{16,24},{24,32},{32,40},{40,48},{48,56},{56,64},{64,7... | collective-permute-start | bytes 4832 | tf_op jit(solution)/shard_map/ppermute | solution.py:20
  104.9 1.1 select_bitcast_fusion
  106.2 2.7 %fusion.7 = f32[3,256,64]{2,0,1:T(4,128)S(1)} fusion(bf16[64,256,128]{2,1,0:T(8,128)(2,1)S(1)} %bitcast.150, bf16[3,256,128]{2,1,0:T(8,128)(2,1)S(1)} %fusion.12), kind=kOutput, calls=%fused_computation.8 | convolution fusion | flops 12582912 | bytes 4587520 | tf_op jit(solution)/shard_map/brj,qrj->qrb/dot_general | solution.py:226
  110.1 4.3 %collective-permute-start.11 = (f32[128,3,128]{2,1,0:T(4,128)S(1)}, f32[128,3,128]{2,1,0:T(4,128)S(1)}, u32[]{:S(2)}, u32[]{:S(2)}) collective-permute-start(f32[128,3,128]{2,1,0:T(4,128)S(1)} %pad_maximum_fusion.1), channel_id=1, source_target_pairs={{128,0},{129,1},{130,2},{131,3},{132,4},{133,5},{134,6},{135,7},{1... | collective-permute-start | bytes 589832 | tf_op jit(solution)/shard_map/ppermute | solution.py:235
  115.7 28.6 %all_to_all.21.value_ref = f32[128,3,128]{2,1,0:T(4,128)} all-to-all(f32[128,3,128]{2,1,0:T(4,128)S(1)} %maximum_select_fusion), channel_id=1, replica_groups=mesh['grp'=2,'gx'=16,'gy'=8] {'gx','gy'}, dimensions={0} | all-to-all | bytes 393216 | tf_op jit(solution)/shard_map/all_to_all | solution.py:236
  144.4 6.0 %scatter.1 = f32[24,256]{1,0:T(8,128)} custom-call(s32[128,128]{1,0:T(8,128)} %bitcast.171, f32[128,3,128]{2,1,0:T(4,128)} %all_to_all.21.value_ref), custom_call_target="tpu_custom_call" | custom-call | tf_op jit(solution)/shard_map/scatter/pallas_call | solution.py:115
  150.3 3.8 %collective-permute-start.12 = (f32[24,256]{1,0:T(8,128)}, f32[24,256]{1,0:T(8,128)S(1)}, u32[]{:S(2)}, u32[]{:S(2)}) collective-permute-start(f32[24,256]{1,0:T(8,128)} %scatter.1), channel_id=1, source_target_pairs={{128,0},{129,1},{130,2},{131,3},{132,4},{133,5},{134,6},{135,7},{1... | collective-permute-start | bytes 73736 | tf_op jit(solution)/shard_map/ppermute | solution.py:238
  154.1 1.0 collective-permute-done.12
  (78 shorter events, 17.1 us)
Async XLA Ops:
  0.6 11.8 %copy-start.5 = (f32[1,256,128]{2,1,0:T(8,128)S(1)}, f32[1,256,128]{2,1,0:T(8,128)}, u32[]{:S(2)}) copy-start(f32[1,256,128]{2,1,0:T(8,128)} %param.16) | copy-start | bytes 393220
  0.6 15.2 %copy-start = (bf16[1,64,256,128]{3,2,1,0:T(8,128)(2,1)S(1)}, bf16[1,64,256,128]{3,2,1,0:T(8,128)(2,1)}, u32[]{:S(2)}) copy-start(bf16[1,64,256,128]{3,2,1,0:T(8,128)(2,1)} %param.10) | copy-start | bytes 12582916
  3.2 13.3 %collective-permute-start = (s32[128,128]{0,1:T(8,128)S(1)}, s32[128,128]{0,1:T(8,128)S(1)}, u32[]{:S(2)}, u32[]{:S(2)}) collective-permute-start(s32[128,128]{0,1:T(8,128)S(1)} %pad_add_fusion.1), channel_id=1, source_target_pairs={{128,0},{129,1},{130,2},{131,3},{132,4},{133,5},{134,6},{135,7},{1... | collective-permute-start | bytes 196616 | tf_op jit(solution)/shard_map/ppermute | solution.py:170
  9.3 25.0 %collective-permute-start.5 = (bf16[128,256]{1,0:T(8,128)(2,1)S(1)}, bf16[128,256]{1,0:T(8,128)(2,1)S(1)}, u32[]{:S(2)}, u32[]{:S(2)}) collective-permute-start(bf16[128,256]{1,0:T(8,128)(2,1)S(1)} %bitcast.176), channel_id=1, source_target_pairs={{0,128},{1,129},{2,130},{3,131},{4,132},{5,133},{6,134},{7,135},{8... | collective-permute-start | bytes 196616 | tf_op jit(solution)/shard_map/ppermute | solution.py:157
  12.7 46.8 %collective-permute-start.1 = (f32[3,4,256]{1,2,0:T(8,128)S(1)}, f32[3,4,256]{1,2,0:T(8,128)S(1)}, u32[]{:S(2)}, u32[]{:S(2)}) collective-permute-start(f32[3,4,256]{1,2,0:T(8,128)S(1)} %get-tuple-element.22), channel_id=1, source_target_pairs={{0,1},{1,2},{2,3},{3,4},{4,5},{5,6},{6,7},{8,9},{9,10},{10,11},{11... | collective-permute-start | bytes 36872 | tf_op jit(solution)/shard_map/ppermute | solution.py:20
  14.5 44.9 %collective-permute-start.2 = (f32[3,4,256]{1,2,0:T(8,128)S(1)}, f32[3,4,256]{1,2,0:T(8,128)S(1)}, u32[]{:S(2)}, u32[]{:S(2)}) collective-permute-start(f32[3,4,256]{1,2,0:T(8,128)S(1)} %get-tuple-element.23), channel_id=1, source_target_pairs={{1,0},{2,1},{3,2},{4,3},{5,4},{6,5},{7,6},{9,8},{10,9},{11,10},{12... | collective-permute-start | bytes 36872 | tf_op jit(solution)/shard_map/ppermute | solution.py:21
  17.2 27.7 %all-to-all-start = ((s32[128,1,128]{2,1,0:T(1,128)}), s32[128,1,128]{2,1,0:T(1,128)S(1)}, u32[]{:S(2)}, u32[]{:S(2)}) async-start(s32[128,1,128]{2,1,0:T(1,128)} %copy.29), calls=%async_computation | async-start | bytes 131072 | tf_op jit(solution)/shard_map/all_to_all | solution.py:171
  44.9 0.6 copy-start.2
  53.2 19.5 %all-to-all-start.1 = ((bf16[128,5,2,128]{3,2,1,0:T(2,128)(2,1)}), bf16[128,5,2,128]{3,2,1,0:T(2,128)(2,1)S(1)}, u32[]{:S(2)}, u32[]{:S(2)}) async-start(bf16[128,5,2,128]{3,2,1,0:T(2,128)(2,1)} %copy.32), calls=%async_computation.1 | async-start | bytes 655360 | tf_op jit(solution)/shard_map/all_to_all | solution.py:175
  59.5 3.9 %collective-permute-start.3 = (f32[3,4,136]{2,1,0:T(4,128)S(1)}, f32[3,4,136]{2,1,0:T(4,128)S(1)}, u32[]{:S(2)}, u32[]{:S(2)}) collective-permute-start(f32[3,4,136]{2,1,0:T(4,128)S(1)} %get-tuple-element.11), channel_id=1, source_target_pairs={{0,8},{8,16},{16,24},{24,32},{32,40},{40,48},{48,56},{56,64},{64,7... | collective-permute-start | bytes 19592 | tf_op jit(solution)/shard_map/ppermute | solution.py:20
  62.0 4.8 %collective-permute-start.4 = (f32[3,4,136]{2,1,0:T(4,128)S(1)}, f32[3,4,136]{2,1,0:T(4,128)S(1)}, u32[]{:S(2)}, u32[]{:S(2)}) collective-permute-start(f32[3,4,136]{2,1,0:T(4,128)S(1)} %get-tuple-element.12), channel_id=1, source_target_pairs={{8,0},{16,8},{24,16},{32,24},{40,32},{48,40},{56,48},{64,56},{72,6... | collective-permute-start | bytes 19592 | tf_op jit(solution)/shard_map/ppermute | solution.py:21
  73.4 6.6 %collective-permute-start.6 = (bf16[128,10,2,64]{0,3,2,1:T(8,128)(2,1)S(1)}, bf16[128,10,2,64]{0,3,2,1:T(8,128)(2,1)S(1)}, u32[]{:S(2)}, u32[]{:S(2)}) collective-permute-start(bf16[128,10,2,64]{0,3,2,1:T(8,128)(2,1)S(1)} %bitcast.159), channel_id=1, source_target_pairs={{0,128},{1,129},{2,130},{3,131},{4,132},{5,133},{6,134},{7,135},{8... | collective-permute-start | bytes 983048 | tf_op jit(solution)/shard_map/ppermute | solution.py:177
  74.9 6.8 %copy-start.6 = (s32[1,256,128]{2,1,0:T(8,128)S(1)}, s32[1,256,128]{2,1,0:T(8,128)}, u32[]{:S(2)}) copy-start(s32[1,256,128]{2,1,0:T(8,128)} %param.13) | copy-start | bytes 393220
  80.8 6.3 %copy-start.4 = (s32[1,256,128]{2,1,0:T(8,128)S(1)}, s32[1,256,128]{2,1,0:T(8,128)}, u32[]{:S(2)}) copy-start(s32[1,256,128]{2,1,0:T(8,128)} %param.14) | copy-start | bytes 393220
  87.2 4.8 %collective-permute-start.7 = (f32[1,3,256]{1,2,0:T(8,128)S(1)}, f32[1,3,256]{1,2,0:T(8,128)S(1)}, u32[]{:S(2)}, u32[]{:S(2)}) collective-permute-start(f32[1,3,256]{1,2,0:T(8,128)S(1)} %get-tuple-element.34), channel_id=1, source_target_pairs={{0,1},{1,2},{2,3},{3,4},{4,5},{5,6},{6,7},{8,9},{9,10},{10,11},{11... | collective-permute-start | bytes 9224 | tf_op jit(solution)/shard_map/ppermute | solution.py:20
  89.3 6.5 %collective-permute-start.8 = (f32[1,3,256]{1,2,0:T(8,128)S(1)}, f32[1,3,256]{1,2,0:T(8,128)S(1)}, u32[]{:S(2)}, u32[]{:S(2)}) collective-permute-start(f32[1,3,256]{1,2,0:T(8,128)S(1)} %get-tuple-element.35), channel_id=1, source_target_pairs={{1,0},{2,1},{3,2},{4,3},{5,4},{6,5},{7,6},{9,8},{10,9},{11,10},{12... | collective-permute-start | bytes 9224 | tf_op jit(solution)/shard_map/ppermute | solution.py:21
  95.9 5.5 %collective-permute-start.10 = (f32[1,3,134]{2,1,0:T(4,128)S(1)}, f32[1,3,134]{2,1,0:T(4,128)S(1)}, u32[]{:S(2)}, u32[]{:S(2)}) collective-permute-start(f32[1,3,134]{2,1,0:T(4,128)S(1)} %get-tuple-element.21), channel_id=1, source_target_pairs={{8,0},{16,8},{24,16},{32,24},{40,32},{48,40},{56,48},{64,56},{72,6... | collective-permute-start | bytes 4832 | tf_op jit(solution)/shard_map/ppermute | solution.py:21
  97.2 4.7 %collective-permute-start.9 = (f32[1,3,134]{2,1,0:T(4,128)S(1)}, f32[1,3,134]{2,1,0:T(4,128)S(1)}, u32[]{:S(2)}, u32[]{:S(2)}) collective-permute-start(f32[1,3,134]{2,1,0:T(4,128)S(1)} %get-tuple-element.20), channel_id=1, source_target_pairs={{0,8},{8,16},{16,24},{24,32},{32,40},{40,48},{48,56},{56,64},{64,7... | collective-permute-start | bytes 4832 | tf_op jit(solution)/shard_map/ppermute | solution.py:20
  103.9 2.2 %copy-start.3 = (f32[1,256,128]{2,1,0:T(8,128)S(1)}, f32[1,256,128]{2,1,0:T(8,128)}, u32[]{:S(2)}) copy-start(f32[1,256,128]{2,1,0:T(8,128)} %param.15) | copy-start | bytes 393220
  103.9 2.3 %copy-start.1 = (bf16[1,64,256,128]{3,2,1,0:T(8,128)(2,1)S(1)}, bf16[1,64,256,128]{3,2,1,0:T(8,128)(2,1)}, u32[]{:S(2)}) copy-start(bf16[1,64,256,128]{3,2,1,0:T(8,128)(2,1)} %param.10) | copy-start | bytes 12582916
  110.1 5.5 %collective-permute-start.11 = (f32[128,3,128]{2,1,0:T(4,128)S(1)}, f32[128,3,128]{2,1,0:T(4,128)S(1)}, u32[]{:S(2)}, u32[]{:S(2)}) collective-permute-start(f32[128,3,128]{2,1,0:T(4,128)S(1)} %pad_maximum_fusion.1), channel_id=1, source_target_pairs={{128,0},{129,1},{130,2},{131,3},{132,4},{133,5},{134,6},{135,7},{1... | collective-permute-start | bytes 589832 | tf_op jit(solution)/shard_map/ppermute | solution.py:235
  150.3 4.8 %collective-permute-start.12 = (f32[24,256]{1,0:T(8,128)}, f32[24,256]{1,0:T(8,128)S(1)}, u32[]{:S(2)}, u32[]{:S(2)}) collective-permute-start(f32[24,256]{1,0:T(8,128)} %scatter.1), channel_id=1, source_target_pairs={{128,0},{129,1},{130,2},{131,3},{132,4},{133,5},{134,6},{135,7},{1... | collective-permute-start | bytes 73736 | tf_op jit(solution)/shard_map/ppermute | solution.py:238

commit v2 on v1

v2 whole, which is shorter than its diff:
```python
import jax
import jax.numpy as jnp
from jax import lax
from jax.experimental import pallas as pl
from jax.experimental.pallas import tpu as pltpu
from jax.sharding import PartitionSpec as P

STEPS = 4
SMB_RATE = 0.5
LOW = 256
EDGE = 8
PLANES = ("gx", "gy")
F32 = jnp.float32
BF16 = jnp.bfloat16
EXACT = lax.Precision.HIGHEST
ROOM = pltpu.CompilerParams(vmem_limit_bytes=16 << 20)


def swap_cores(value):
    return lax.ppermute(value, "grp", [(0, 1), (1, 0)])


def ring(value, axis, step):
    count = lax.axis_size(axis)
    return lax.ppermute(value, axis, [(i, (i + step) % count) for i in range(count)])


def after(value, *others):
    return lax.optimization_barrier((value,) + others)[0]


def ones_where(mask):
    return jnp.where(mask, 1.0, 0.0).astype(BF16)


def head_kernel(owner_ref, rows_ref, low_ref, high_ref, place_ref):
    groups, row_count = low_ref.shape[0], owner_ref.shape[1]
    width = rows_ref.shape[0]
    named = lax.broadcasted_iota(jnp.int32, (groups, row_count), 0) == owner_ref[...]
    square = (row_count, row_count)
    earlier = lax.broadcasted_iota(jnp.int32, square, 0) < lax.broadcasted_iota(
        jnp.int32, square, 1
    )
    rank = jnp.dot(ones_where(named), ones_where(earlier), preferred_element_type=F32)
    rank = jnp.where(named, rank, -1.0)
    rows = rows_ref[...]
    digits = jnp.concatenate([rows >> 3, rows & 7], axis=0).astype(F32).astype(BF16)
    for half, out_ref in enumerate((low_ref, high_ref)):
        parts = []
        for k in (2 * half, 2 * half + 1):
            mine = ones_where(rank == k)
            place_ref[groups * k : groups * (k + 1), :] = mine
            found = lax.dot_general(
                mine, digits, (((1,), (1,)), ((), ())), preferred_element_type=F32
            )
            parts.append(8.0 * found[:, :width] + found[:, width:])
        out_ref[...] = jnp.concatenate(parts, axis=1).astype(jnp.int32)


def head(owner_row, rows, groups):
    row_count = owner_row.shape[1]
    lanes = 2 * rows.shape[0]
    return pl.pallas_call(
        head_kernel,
        out_shape=(
            jax.ShapeDtypeStruct((groups, lanes), jnp.int32),
            jax.ShapeDtypeStruct((groups, lanes), jnp.int32),
            jax.ShapeDtypeStruct((4 * groups, row_count), BF16),
        ),
        compiler_params=ROOM,
        name="head",
    )(owner_row, rows)


def hot_low(low, tiles):
    key = jnp.broadcast_to(low.astype(F32), (16, 128)).astype(BF16)
    one = jnp.ones((16, 128), BF16)
    zero = jnp.zeros((16, 128), BF16)
    return jnp.concatenate([jnp.where(tile == key, one, zero) for tile in tiles], axis=0)


def low_tiles():
    base = lax.broadcasted_iota(jnp.int32, (16, 128), 0)
    return [(base + 16 * i).astype(F32).astype(BF16) for i in range(LOW // 16)]


def pick_kernel(table_ref, index_ref, out_ref):
    sources = index_ref.shape[0]
    high_count = table_ref.shape[0] // 16
    table = table_ref[...]
    tiles = low_tiles()
    group = min(32, sources)

    def pick_group(i, carry):
        start = pl.multiple_of(i * group, group)
        block = index_ref[pl.ds(start, group), :]
        for s in range(0, group, 2):
            rows = [block[s + d : s + d + 1, :] for d in range(2)]
            hot = jnp.concatenate([hot_low(row & (LOW - 1), tiles) for row in rows], axis=1)
            found = jnp.dot(table, hot, preferred_element_type=F32)
            for d in range(2):
                high = jnp.broadcast_to(rows[d] // LOW, (16, 128))
                part = found[:, 128 * d : 128 * d + 128]
                total = part[:16]
                for h in range(1, high_count):
                    total = jnp.where(high == h, part[16 * h : 16 * h + 16], total)
                total = total.astype(BF16)
                for pair in range(out_ref.shape[1]):
                    out_ref[start + s + d, pair] = total[2 * pair : 2 * pair + 2]
        return carry

    lax.fori_loop(0, sources // group, pick_group, 0)


def pick(table, asked, classes):
    return pl.pallas_call(
        pick_kernel,
        out_shape=jax.ShapeDtypeStruct((asked.shape[0], classes // 2, 2, 128), BF16),
        compiler_params=ROOM,
        name="pick",
    )(table, asked)


def scatter_kernel(index_ref, value_ref, out_ref):
    sources = index_ref.shape[0]
    high_count = out_ref.shape[0] // 3
    tiles = low_tiles()
    high_iota = lax.broadcasted_iota(jnp.int32, (high_count, 128), 0)
    group = min(64, sources)

    def add_group(i, total):
        start = pl.multiple_of(i * group, group)
        block = index_ref[pl.ds(start, group), :]
        hot = []
        spread = []
        for s in range(group):
            row = block[s : s + 1, :]
            hot.append(hot_low(row & (LOW - 1), tiles))
            mine = high_iota == row // LOW
            values = value_ref[start + s]
            first = values.astype(BF16).astype(F32)
            rows = []
            for part in (first, values - first):
                for q in range(3):
                    rows.append(jnp.where(mine, part[q : q + 1], 0.0))
            spread.append(jnp.concatenate(rows, axis=0).astype(BF16))
        sums = lax.dot_general(
            jnp.concatenate(spread, axis=1),
            jnp.concatenate(hot, axis=1),
            (((1,), (1,)), ((), ())),
            preferred_element_type=F32,
        )
        return total + (sums[: 3 * high_count] + sums[3 * high_count :])

    out_ref[...] = lax.fori_loop(
        0, sources // group, add_group, jnp.zeros(out_ref.shape, F32)
    )


def scatter(asked, values, high_count):
    return pl.pallas_call(
        scatter_kernel,
        out_shape=jax.ShapeDtypeStruct((3 * high_count, LOW), F32),
        compiler_params=ROOM,
        name="scatter",
    )(asked, values)


LANE_GATHER = lax.GatherDimensionNumbers(
    offset_dims=(),
    collapsed_slice_dims=(1,),
    start_index_map=(1,),
    operand_batching_dims=(0,),
    start_indices_batching_dims=(0,),
)


def lanes_at(values, lanes):
    return lax.gather(
        values,
        lanes[..., None],
        LANE_GATHER,
        slice_sizes=(1, 1),
        mode=lax.GatherScatterMode.PROMISE_IN_BOUNDS,
    )


def remap_kernel(
    near_ref, far_ref, place_ref, order_ref, weight_ref, class_ref, mask_ref,
    source_ref, total_ref, left_ref, right_ref, table_ref,
):
    width, row_count, cols = weight_ref.shape
    groups = near_ref.shape[0]
    classes = near_ref.shape[1] // 128

    answers = jnp.concatenate([near_ref[...], far_ref[...]], axis=0)
    both = []
    for parity in range(2):
        place = jnp.concatenate(
            [place_ref[groups * k : groups * (k + 1), :] for k in (parity, parity + 2)],
            axis=0,
        )
        both.append(
            lax.dot_general(
                place, answers, (((0,), (0,)), ((), ())), preferred_element_type=F32
            )
        )
    lower = lax.broadcasted_iota(jnp.int32, (row_count, 128), 1) < 64
    picked = []
    for e in range(0, classes, 2):
        here, there = [
            [array[:, 128 * c : 128 * c + 128] for array in both] for c in (e, e + 1)
        ]
        picked.append(
            jnp.where(
                lower,
                here[0] + pltpu.roll(here[1], 64, 1),
                pltpu.roll(there[0], 64, 1) + there[1],
            ).astype(BF16)
        )
    table_ref[...] = jnp.dot(
        jnp.concatenate(picked, axis=1), order_ref[...], preferred_element_type=F32
    ).astype(BF16)

    tile = min(32, row_count)

    def remap_rows(i, carry):
        rows = pl.ds(pl.multiple_of(i * tile, tile), tile)
        chosen = (class_ref[rows, :] * 8).astype(jnp.int16)
        total = jnp.zeros((tile, cols), F32)
        found = [jnp.zeros((tile, cols), F32)] * 2
        for g in range(width // 8):
            part = table_ref[rows, 128 * g : 128 * g + 128]
            for b in range(8):
                weight = weight_ref[8 * g + b, rows, :].astype(F32)
                value = lanes_at(part, chosen + jnp.asarray(b, jnp.int16)).astype(F32)
                found[b % 2] = found[b % 2] + weight * value
                total = total + weight
        total_ref[rows, :] = total
        source_ref[rows, :] = mask_ref[rows, :].astype(F32) * (
            (found[0] + found[1]) / total
        )
        return carry

    lax.fori_loop(0, row_count // tile, remap_rows, 0)

    lane = lax.broadcasted_iota(jnp.int32, (EDGE, cols), 1)
    line = lax.broadcasted_iota(jnp.int32, (EDGE, cols), 0)
    for out_ref, offset in ((left_ref, 0), (right_ref, cols - EDGE)):
        out_ref[...] = lax.dot_general(
            jnp.where(lane == line + offset, 1.0, 0.0),
            source_ref[...],
            (((1,), (1,)), ((), ())),
            precision=EXACT,
            preferred_element_type=F32,
        )


def remap(near, far, place, order, weights, classes, mask):
    row_count, cols = weights.shape[1:]
    plane = jax.ShapeDtypeStruct((row_count, cols), F32)
    edge = jax.ShapeDtypeStruct((EDGE, row_count), F32)
    return pl.pallas_call(
        remap_kernel,
        out_shape=(plane, plane, edge, edge),
        scratch_shapes=[pltpu.VMEM((row_count, order.shape[1]), BF16)],
        compiler_params=ROOM,
        name="remap",
    )(near, far, place, order, weights, classes, mask)


def side_kernel(source_ref, low_ref, high_ref, side_ref, top_ref, bottom_ref):
    row_count, cols = source_ref.shape
    lane = lax.broadcasted_iota(jnp.int32, (2 * EDGE, cols), 1)
    line = lax.broadcasted_iota(jnp.int32, (2 * EDGE, cols), 0)
    spot = jnp.where(line < EDGE, line, line + cols - 2 * EDGE)
    side = lax.dot_general(
        jnp.concatenate([high_ref[...], low_ref[...]], axis=0),
        jnp.where(lane == spot, 1.0, 0.0),
        (((0,), (0,)), ((), ())),
        precision=EXACT,
        preferred_element_type=F32,
    )
    side_ref[...] = side
    for out_ref, first in ((top_ref, 0), (bottom_ref, row_count - EDGE)):
        out_ref[:, :cols] = source_ref[first : first + EDGE, :]
        out_ref[:, cols:] = side[first : first + EDGE, :]


def side(source, from_low, from_high):
    row_count, cols = source.shape
    return pl.pallas_call(
        side_kernel,
        out_shape=(
            jax.ShapeDtypeStruct((row_count, cols), F32),
            jax.ShapeDtypeStruct((EDGE, 2 * cols), F32),
            jax.ShapeDtypeStruct((EDGE, 2 * cols), F32),
        ),
        compiler_params=ROOM,
        name="side",
    )(source, from_low, from_high)


def relax_kernel(
    source_ref, side_ref, above_ref, below_ref, fixed_ref, inside_ref, total_ref, mask_ref,
    thick_ref, field_ref,
):
    row_count, cols = source_ref.shape
    rows, lanes = inside_ref.shape
    ahead = lambda a, axis: pltpu.roll(a, (rows, lanes)[axis] - 1, axis)
    back = lambda a, axis: pltpu.roll(a, 1, axis)
    source = SMB_RATE * jnp.concatenate(
        [
            above_ref[...],
            jnp.concatenate([source_ref[...], side_ref[...]], axis=1),
            below_ref[...],
        ],
        axis=0,
    )
    bed, diff, thick = fixed_ref[0], fixed_ref[1], fixed_ref[2]
    inside = inside_ref[...]
    gain = [0.5 * (diff + ahead(diff, axis)) for axis in range(2)]
    for step in range(STEPS):
        surface = bed + thick
        change = source
        for axis in range(2):
            flow = gain[axis] * (ahead(surface, axis) - surface)
            change = change + (flow - back(flow, axis))
        thick = jnp.maximum(thick + change, 0.0) * inside
    own = thick[EDGE : EDGE + row_count, :cols]
    thick_ref[...] = own
    total = total_ref[...]
    field_ref[0] = ((bed[EDGE : EDGE + row_count, :cols] + own) / total).astype(BF16)
    field_ref[1] = (mask_ref[...].astype(F32) * jnp.minimum(own, 1.0) / total).astype(BF16)
    field_ref[2] = (1.0 / total).astype(BF16)


def relax(source, side_tile, above, below, fixed, inside, total, mask):
    return pl.pallas_call(
        relax_kernel,
        out_shape=(
            jax.ShapeDtypeStruct(source.shape, F32),
            jax.ShapeDtypeStruct((3,) + source.shape, BF16),
        ),
        compiler_params=ROOM,
        name="relax",
    )(source, side_tile, above, below, fixed, inside, total, mask)


def per_device(
    fluxes, weights, land_rows, owners, elev_class, ice_mask, bed, thickness, diffusivity
):
    groups = lax.axis_size("gx") * lax.axis_size("gy")
    is_ice = lax.axis_index("grp") == 1
    block_weights = weights[0]
    width, row_count, cols = block_weights.shape
    classes, cells = fluxes.shape[1:]
    high_count = cells // LOW

    low_half, high_half, place = head(
        owners.reshape(1, row_count), jnp.transpose(land_rows[0]), groups
    )
    request = jnp.where(is_ice, low_half, swap_cores(high_half))
    asked = lax.all_to_all(request, PLANES, split_axis=0, concat_axis=0, tiled=True)

    flux, fixed = lax.optimization_barrier(
        (fluxes[0], jnp.stack([bed[0], diffusivity[0], thickness[0]]), request)
    )[:2]
    table = jnp.pad(flux.astype(BF16), ((0, 16 - classes), (0, 0)))
    table = jnp.transpose(table.reshape(16, high_count, LOW), (1, 0, 2)).reshape(-1, LOW)
    table = jnp.where(is_ice, swap_cores(table), table)
    turn = lambda part: jnp.transpose(part, (0, 2, 1))
    from_low = turn(ring(turn(fixed[:, :, cols - STEPS :]), "gy", 1))
    from_high = turn(ring(turn(fixed[:, :, :STEPS]), "gy", -1))
    fixed = jnp.concatenate(
        [fixed, from_high, jnp.zeros((3, row_count, cols - 2 * STEPS), F32), from_low], axis=2
    )

    row_at = lax.broadcasted_iota(jnp.int32, (row_count + 2 * EDGE, 2 * cols), 0) - EDGE
    col_at = lax.broadcasted_iota(jnp.int32, (row_count + 2 * EDGE, 2 * cols), 1)
    col_at = jnp.where(col_at < cols + cols // 2, col_at, col_at - 2 * cols)
    at_x, at_y = lax.axis_index("gx"), lax.axis_index("gy")
    inside = (
        ((row_at >= 0) | (at_x > 0))
        & ((row_at < row_count) | (at_x < lax.axis_size("gx") - 1))
        & ((col_at >= 0) | (at_y > 0))
        & ((col_at < cols) | (at_y < lax.axis_size("gy") - 1))
    ).astype(F32)
    line = lax.broadcasted_iota(jnp.int32, (classes * width, 16 * width), 0)
    lane = lax.broadcasted_iota(jnp.int32, (classes * width, 16 * width), 1)
    order = (
        (lane // 128 == line % width // 8)
        & (lane % 128 // 8 == line // width)
        & (lane % 8 == line % 8)
    ).astype(BF16)

    asked, fixed, order, inside = lax.optimization_barrier((asked, fixed, order, inside))
    answer = pick(table, asked, classes)
    near = lax.all_to_all(answer, PLANES, split_axis=0, concat_axis=0, tiled=True)

    fixed = after(fixed, answer)
    above = ring(fixed[:, row_count - EDGE :], "gx", 1)
    below = ring(fixed[:, :EDGE], "gx", -1)
    fixed = jnp.concatenate([above, fixed, below], axis=1) * inside
    near, fixed = lax.optimization_barrier((near, fixed))

    near = near.reshape(groups, classes * 128)
    source, total, left, right = remap(
        near, swap_cores(near), place, order, block_weights, elev_class[0], ice_mask[0]
    )
    side_tile, top, bottom = side(source, ring(right, "gy", 1), ring(left, "gy", -1))
    thick, fields = relax(
        source,
        side_tile,
        ring(bottom, "gx", 1),
        ring(top, "gx", -1),
        fixed,
        inside,
        total,
        ice_mask[0],
    )

    partial = jnp.einsum("brj,qrj->qrb", block_weights, fields, preferred_element_type=F32)
    outgoing = jnp.einsum(
        "kor,qrb->koqb",
        place.reshape(4, groups, row_count).astype(F32),
        partial,
        precision=EXACT,
        preferred_element_type=F32,
    )
    outgoing = [jnp.concatenate([outgoing[k], outgoing[k + 1]], axis=2) for k in (0, 2)]
    sent = jnp.where(is_ice, outgoing[0], swap_cores(outgoing[1]))
    arrived = lax.all_to_all(sent, PLANES, split_axis=0, concat_axis=0, tiled=True)
    land_sums = scatter(asked, arrived, high_count)
    land_sums = (land_sums + swap_cores(land_sums)).reshape(3, cells)
    averaged = land_sums[:2] / jnp.maximum(land_sums[2], 1.0)
    land_fields = jnp.where(is_ice, 0.0, averaged)[None]
    thickness_new = jnp.where(is_ice, thick, 0.0)[None]
    return (land_fields, thickness_new)


def solution(mesh):
    return jax.shard_map(
        per_device,
        mesh=mesh,
        in_specs=(
            P("grp", None, ("gx", "gy")),
            P("grp", None, "gx", "gy"),
            P("grp", "gx", "gy"),
            P("grp", "gx", "gy", None, None),
            P("grp", "gx", "gy"),
            P("grp", "gx", "gy"),
            P("grp", "gx", "gy"),
            P("grp", "gx", "gy"),
            P("grp", "gx", "gy"),
        ),
        out_specs=(P("grp", None, ("gx", "gy")), P("grp", "gx", "gy")),
        check_vma=False,
    )
```

time: 158 us -> 125 us (0.79)
  waiting for transfers between devices: 30.8 us -> 18.4 us
  matrix products: 10.6 us -> 3.11 us
  starting transfers between devices: 55.1 us -> 47.7 us
  blocking collectives: 28.6 us -> 25.2 us
  other arithmetic: 10.3 us -> 8.37 us
    ppermute x13, waiting for transfers between devices: 15.4 us -> 6.02 us  [the longest x8 3.72 us: ring(): lax.ppermute(value, axis, [(i, (i + step) % count) for i in range(count)])]
    dot_general x4 -> x1, matrix products: 7.04 us -> 0.42 us  [per_device(): jnp.einsum('kor,qrb->koqb', place.reshape(4, groups, row_count).astype(F3...]
    all_to_all x1, starting transfers between devices: 17.1 us -> 11.4 us  [per_device(): lax.all_to_all(request, PLANES, split_axis=0, concat_axis=0, tiled=True)]
    add x5 -> x3, other arithmetic: 3.71 us -> 0.01 us  [the longest x1 0.01 us: per_device(): line % 8]
    all_to_all x1, blocking collectives: 28.6 us -> 25.2 us  [per_device(): lax.all_to_all(sent, PLANES, split_axis=0, concat_axis=0, tiled=True)]
    ppermute x13, starting transfers between devices: 31.7 us -> 29 us  [the longest x8 16.3 us: ring(): lax.ppermute(value, axis, [(i, (i + step) % count) for i in range(count)])]
    all_to_all x1, waiting for transfers between devices: 9.87 us -> 7.29 us  [per_device(): lax.all_to_all(request, PLANES, split_axis=0, concat_axis=0, tiled=True)]
    unnamed x22 -> x18, local copies, waits for them, and re-layouts: 3.11 us -> 5.23 us
  transfers between devices with their start and end apart: 15 -> 15, of which waited for: 9 -> 8; matrix products, arithmetic and copies ran while one was open for 6% -> 7% of each run, Pallas kernels for 4% -> 0%
where the time goes in v2:
time: 125 us; the launch traced here: 124 us
  starting transfers between devices  47.7 us (38%)
  blocking collectives  25.2 us (20%)
  waiting for transfers between devices  18.4 us (15%)
  Pallas kernels  12.2 us (10%)
  other arithmetic  8.37 us (7%)
  local copies, waits for them, and re-layouts  8.27 us (7%)
  matrix products  3.11 us (2%)
    all_to_all x1, blocking collectives, per_device(): lax.all_to_all(sent, PLANES, split_axis=0, concat_axis=0, tiled=True)  25.2 us
    ppermute x8, starting transfers between devices, ring(): lax.ppermute(value, axis, [(i, (i + step) % count) for i in range(count)])  16.3 us
    ppermute x5, starting transfers between devices, swap_cores(): return lax.ppermute(value, 'grp', [(0, 1), (1, 0)])  12.7 us
    all_to_all x1, starting transfers between devices, per_device(): lax.all_to_all(request, PLANES, split_axis=0, concat_axis=0, tiled=True)  11.4 us
    all_to_all x1, waiting for transfers between devices, per_device(): lax.all_to_all(request, PLANES, split_axis=0, concat_axis=0, tiled=True)  7.29 us
    all_to_all x1, starting transfers between devices, per_device(): lax.all_to_all(answer, PLANES, split_axis=0, concat_axis=0, tiled=True)  7.23 us
    unnamed x18, local copies, waits for them, and re-layouts  5.23 us
    all_to_all x1, waiting for transfers between devices, per_device(): lax.all_to_all(answer, PLANES, split_axis=0, concat_axis=0, tiled=True)  5.04 us
  transfers between devices with their start and end apart: 15, of which 8 were waited for; matrix products, arithmetic and copies ran while one was open for 7% of the time, Pallas kernels for 0%

profile of v2, /device:TPU:1, one launch (start us, length us, event | category | flops | bytes accessed | tf_op | source)
XLA Modules:
  0.0 124.1 jit_solution(13157401684193246646)
XLA Ops:
  2.7 3.3 %collective-permute-start = (s32[128,128]{1,0:T(8,128)S(1)}, s32[128,128]{1,0:T(8,128)S(1)}, u32[]{:S(2)}, u32[]{:S(2)}) collective-permute-start(s32[128,128]{1,0:T(8,128)S(1)} %get-tuple-element.24), channel_id=1, source_target_pairs={{0,128},{128,0},{1,129},{129,1},{2,130},{130,2},{3,131},{131,3},{4... | collective-permute-start | bytes 196616 | tf_op jit(solution)/shard_map/ppermute | solution.py:20
  6.1 0.9 copy.39
  7.0 1.1 pad_maximum_fusion.1
  8.1 1.3 %fusion.16.order_ref = bf16[640,1024]{1,0:T(8,128)(2,1)S(1)} fusion(s32[640]{0:T(1024)S(1)} %get-tuple-element.52, s32[640]{0:T(1024)S(1)} %get-tuple-element.62, s32[1024]{0:T(1024)S(1)} %get-tuple-element.56, s32[1024]{0:T(1024)S(1)} %get-tuple-element.60, s32[640]{0:T(1024)S(1)} %get-tuple-element.53, s32[640]{0:T(1024)S(1)} %get-tuple-element.63, ...), kind=kLoop, calls=%fused_computation.31 | loop fusion | flops 27525120 | bytes 1355648 | tf_op jit(solution)/shard_map/convert_element_type | solution.py:395
  10.1 0.9 slice_bitcast_fusion.1
  10.9 3.9 %collective-permute-start.1 = (f32[3,4,256]{1,2,0:T(8,128)}, f32[3,4,256]{1,2,0:T(8,128)}, u32[]{:S(2)}, u32[]{:S(2)}) collective-permute-start(f32[3,4,256]{1,2,0:T(8,128)} %get-tuple-element.50), channel_id=1, source_target_pairs={{0,7},{1,0},{2,1},{3,2},{4,3},{5,4},{6,5},{7,6},{8,15},{9,8},{10,9... | collective-permute-start | bytes 36872 | tf_op jit(solution)/shard_map/ppermute | solution.py:25
  15.0 11.4 %all-to-all-start = ((s32[128,1,128]{2,1,0:T(1,128)}), s32[128,1,128]{2,1,0:T(1,128)S(1)}, u32[]{:S(2)}, u32[]{:S(2)}) async-start(s32[128,1,128]{2,1,0:T(1,128)} %bitcast.4), calls=%async_computation | async-start | bytes 131072 | tf_op jit(solution)/shard_map/all_to_all | solution.py:364
  26.5 1.0 collective-permute-start.3
  27.4 2.2 %pad_maximum_fusion = f32[3,256,256]{2,1,0:T(8,128)} fusion(f32[3,256,4]{2,1,0:T(8,128)} %bitcast.9, f32[3,256,4]{2,1,0:T(8,128)} %bitcast.7, f32[3,256,128]{2,1,0:T(8,128)S(1)} %pad_maximum_fusion.1, f32[256]{0:T(256)S(1)} %pad.14.clone), kind=kLoop, calls=%fused_computation.33 | loop fusion | flops 589824 | bytes 1205248 | tf_op jit(solution)/shard_map/concatenate | solution.py:375
  29.7 7.3 %all-to-all-done = s32[128,1,128]{2,1,0:T(1,128)S(1)} async-done(((s32[128,1,128]{2,1,0:T(1,128)}), s32[128,1,128]{2,1,0:T(1,128)S(1)}, u32[]{:S(2)}, u32[]{:S(2)}) %all-to-all-start) | async-done | bytes 65568 | tf_op jit(solution)/shard_map/all_to_all | solution.py:364
  37.0 2.6 %pick.1 = bf16[128,5,2,128]{3,2,1,0:T(2,128)(2,1)} custom-call(bf16[128,256]{1,0:T(8,128)(2,1)S(1)} %broadcast_select_fusion.table_ref, s32[128,128]{1,0:T(8,128)S(1)} %bitcast.51), custom_call_target="tpu_custom_call" | custom-call | tf_op jit(solution)/shard_map/pick/pallas_call | solution.py:116
  39.6 7.2 %all-to-all-start.1 = ((bf16[128,5,2,128]{3,2,1,0:T(2,128)(2,1)}), bf16[128,5,2,128]{3,2,1,0:T(2,128)(2,1)}, u32[]{:S(2)}, u32[]{:S(2)}) async-start(bf16[128,5,2,128]{3,2,1,0:T(2,128)(2,1)} %pick.1), calls=%async_computation.1 | async-start | bytes 655360 | tf_op jit(solution)/shard_map/all_to_all | solution.py:399
  48.1 4.3 %collective-permute-start.5 = (f32[3,8,256]{2,1,0:T(8,128)S(1)}, f32[3,8,256]{2,1,0:T(8,128)S(1)}, u32[]{:S(2)}, u32[]{:S(2)}) collective-permute-start(f32[3,8,256]{2,1,0:T(8,128)S(1)} %get-tuple-element.45), channel_id=1, source_target_pairs={{0,120},{8,0},{16,8},{24,16},{32,24},{40,32},{48,40},{56,48},{64,5... | collective-permute-start | bytes 73736 | tf_op jit(solution)/shard_map/ppermute | solution.py:25
  52.4 1.6 %collective-permute-done.4 = f32[3,8,256]{2,1,0:T(8,128)S(1)} collective-permute-done((f32[3,8,256]{2,1,0:T(8,128)S(1)}, f32[3,8,256]{2,1,0:T(8,128)S(1)}, u32[]{:S(2)}, u32[]{:S(2)}) %collective-permute-start.4) | collective-permute-done | bytes 24608 | tf_op jit(solution)/shard_map/ppermute | solution.py:25
  54.1 1.2 maximum_multiply_fusion.fixed_ref
  55.3 5.0 %all-to-all-done.1 = bf16[128,5,2,128]{3,2,1,0:T(2,128)(2,1)} async-done(((bf16[128,5,2,128]{3,2,1,0:T(2,128)(2,1)}), bf16[128,5,2,128]{3,2,1,0:T(2,128)(2,1)}, u32[]{:S(2)}, u32[]{:S(2)}) %all-to-all-start.1) | async-done | bytes 327712 | tf_op jit(solution)/shard_map/all_to_all | solution.py:399
  60.3 1.1 reshape.71.near_ref
  61.4 3.7 %collective-permute-start.6 = (bf16[128,1280]{1,0:T(8,128)(2,1)S(1)}, bf16[128,1280]{1,0:T(8,128)(2,1)S(1)}, u32[]{:S(2)}, u32[]{:S(2)}) collective-permute-start(bf16[128,1280]{1,0:T(8,128)(2,1)S(1)} %reshape.71.near_ref), channel_id=1, source_target_pairs={{0,128},{128,0},{1,129},{129,1},{2,130},{130,2},{3,131},{131,3},{4... | collective-permute-start | bytes 983048 | tf_op jit(solution)/shard_map/ppermute | solution.py:20
  65.1 1.3 %collective-permute-done.6.far_ref = bf16[128,1280]{1,0:T(8,128)(2,1)S(1)} collective-permute-done((bf16[128,1280]{1,0:T(8,128)(2,1)S(1)}, bf16[128,1280]{1,0:T(8,128)(2,1)S(1)}, u32[]{:S(2)}, u32[]{:S(2)}) %collective-permute-start.6) | collective-permute-done | bytes 327712 | tf_op jit(solution)/shard_map/ppermute | solution.py:20
  66.4 2.2 %copy-done = bf16[1,64,256,128]{3,2,1,0:T(8,128)(2,1)S(1)} copy-done((bf16[1,64,256,128]{3,2,1,0:T(8,128)(2,1)S(1)}, bf16[1,64,256,128]{3,2,1,0:T(8,128)(2,1)}, u32[]{:S(2)}) %copy-start) | copy-done | bytes 4194328
  68.6 4.8 %remap.1 = (f32[256,128]{1,0:T(8,128)S(1)}, f32[256,128]{1,0:T(8,128)S(1)}, f32[8,256]{1,0:T(8,128)S(1)}, f32[8,256]{1,0:T(8,128)S(1)}) custom-call(bf16[128,1280]{1,0:T(8,128)(2,1)S(1)} %reshape.71.near_ref, bf16[128,1280]{1,0:T(8,128)(2,1)S(1)} %collective-permute-done.6.far_ref, bf16[512,256]{1,0:T(8,128)(2,1)S(1)} %get-tuple-element.27.place_ref, ...), custom_call_target="tpu_custom_call" | custom-call | tf_op jit(solution)/shard_map/remap/pallas_call | solution.py:263
  73.8 2.4 %collective-permute-start.8 = (f32[8,256]{1,0:T(8,128)S(1)}, f32[8,256]{1,0:T(8,128)S(1)}, u32[]{:S(2)}, u32[]{:S(2)}) collective-permute-start(f32[8,256]{1,0:T(8,128)S(1)} %get-tuple-element.36), channel_id=1, source_target_pairs={{0,7},{1,0},{2,1},{3,2},{4,3},{5,4},{6,5},{7,6},{8,15},{9,8},{10,9... | collective-permute-start | bytes 24584 | tf_op jit(solution)/shard_map/ppermute | solution.py:25
  76.2 1.0 collective-permute-done.7.low_ref
  77.7 4.8 %collective-permute-start.10 = (f32[8,256]{1,0:T(8,128)S(1)}, f32[8,256]{1,0:T(8,128)S(1)}, u32[]{:S(2)}, u32[]{:S(2)}) collective-permute-start(f32[8,256]{1,0:T(8,128)S(1)} %get-tuple-element.39), channel_id=1, source_target_pairs={{0,120},{8,0},{16,8},{24,16},{32,24},{40,32},{48,40},{56,48},{64,5... | collective-permute-start | bytes 24584 | tf_op jit(solution)/shard_map/ppermute | solution.py:25
  82.5 1.0 collective-permute-done.9.above_ref
  83.5 1.2 relax.1
  84.7 2.7 %fusion = f32[256,3,64]{2,1,0:T(4,128)S(1)} fusion(bf16[64,256,128]{2,1,0:T(8,128)(2,1)S(1)} %bitcast.49, bf16[3,256,128]{2,1,0:T(8,128)(2,1)S(1)} %get-tuple-element.42), kind=kOutput, calls=%fused_computation.8 | convolution fusion | flops 12582912 | bytes 4587520 | tf_op jit(solution)/shard_map/brj,qrj->qrb/dot_general | solution.py:423
  88.5 2.8 %collective-permute-start.11 = (f32[128,3,128]{2,1,0:T(4,128)S(1)}, f32[128,3,128]{2,1,0:T(4,128)S(1)}, u32[]{:S(2)}, u32[]{:S(2)}) collective-permute-start(f32[128,3,128]{2,1,0:T(4,128)S(1)} %pad_maximum_fusion.2), channel_id=1, source_target_pairs={{0,128},{128,0},{1,129},{129,1},{2,130},{130,2},{3,131},{131,3},{4... | collective-permute-start | bytes 589832 | tf_op jit(solution)/shard_map/ppermute | solution.py:20
  91.6 0.9 collective-permute-done.11
  92.7 25.2 %all_to_all.22.value_ref = f32[128,3,128]{2,1,0:T(4,128)S(1)} all-to-all(f32[128,3,128]{2,1,0:T(4,128)S(1)} %maximum_select_fusion), channel_id=1, replica_groups=mesh['grp'=2,'gx'=16,'gy'=8] {'gx','gy'}, dimensions={0} | all-to-all | bytes 393216 | tf_op jit(solution)/shard_map/all_to_all | solution.py:433
  117.8 2.8 %scatter.1 = f32[24,256]{1,0:T(8,128)S(1)} custom-call(s32[128,128]{1,0:T(8,128)S(1)} %bitcast.52, f32[128,3,128]{2,1,0:T(4,128)S(1)} %all_to_all.22.value_ref), custom_call_target="tpu_custom_call" | custom-call | tf_op jit(solution)/shard_map/scatter/pallas_call | solution.py:161
  120.6 2.0 %collective-permute-start.12 = (f32[24,256]{1,0:T(8,128)S(1)}, f32[24,256]{1,0:T(8,128)S(1)}, u32[]{:S(2)}, u32[]{:S(2)}) collective-permute-start(f32[24,256]{1,0:T(8,128)S(1)} %scatter.1), channel_id=1, source_target_pairs={{0,128},{128,0},{1,129},{129,1},{2,130},{130,2},{3,131},{131,3},{4... | collective-permute-start | bytes 73736 | tf_op jit(solution)/shard_map/ppermute | solution.py:20
  (62 shorter events, 8.2 us)
Async XLA Ops:
  0.6 0.8 copy-start.4
  1.5 0.7 copy-start.5
  2.7 6.8 %collective-permute-start = (s32[128,128]{1,0:T(8,128)S(1)}, s32[128,128]{1,0:T(8,128)S(1)}, u32[]{:S(2)}, u32[]{:S(2)}) collective-permute-start(s32[128,128]{1,0:T(8,128)S(1)} %get-tuple-element.24), channel_id=1, source_target_pairs={{0,128},{128,0},{1,129},{129,1},{2,130},{130,2},{3,131},{131,3},{4... | collective-permute-start | bytes 196616 | tf_op jit(solution)/shard_map/ppermute | solution.py:20
  10.9 16.5 %collective-permute-start.1 = (f32[3,4,256]{1,2,0:T(8,128)}, f32[3,4,256]{1,2,0:T(8,128)}, u32[]{:S(2)}, u32[]{:S(2)}) collective-permute-start(f32[3,4,256]{1,2,0:T(8,128)} %get-tuple-element.50), channel_id=1, source_target_pairs={{0,7},{1,0},{2,1},{3,2},{4,3},{5,4},{6,5},{7,6},{8,15},{9,8},{10,9... | collective-permute-start | bytes 36872 | tf_op jit(solution)/shard_map/ppermute | solution.py:25
  14.8 12.6 %collective-permute-start.2 = (f32[3,4,256]{1,2,0:T(8,128)S(1)}, f32[3,4,256]{1,2,0:T(8,128)}, u32[]{:S(2)}, u32[]{:S(2)}) collective-permute-start(f32[3,4,256]{1,2,0:T(8,128)S(1)} %get-tuple-element.51), channel_id=1, source_target_pairs={{0,1},{1,2},{2,3},{3,4},{4,5},{5,6},{6,7},{7,0},{8,9},{9,10},{10,1... | collective-permute-start | bytes 36872 | tf_op jit(solution)/shard_map/ppermute | solution.py:25
  15.0 21.9 %all-to-all-start = ((s32[128,1,128]{2,1,0:T(1,128)}), s32[128,1,128]{2,1,0:T(1,128)S(1)}, u32[]{:S(2)}, u32[]{:S(2)}) async-start(s32[128,1,128]{2,1,0:T(1,128)} %bitcast.4), calls=%async_computation | async-start | bytes 131072 | tf_op jit(solution)/shard_map/all_to_all | solution.py:364
  26.5 3.2 %collective-permute-start.3 = (bf16[128,256]{1,0:T(8,128)(2,1)S(1)}, bf16[128,256]{1,0:T(8,128)(2,1)S(1)}, u32[]{:S(2)}, u32[]{:S(2)}) collective-permute-start(bf16[128,256]{1,0:T(8,128)(2,1)S(1)} %bitcast.62), channel_id=1, source_target_pairs={{0,128},{128,0},{1,129},{129,1},{2,130},{130,2},{3,131},{131,3},{4... | collective-permute-start | bytes 196616 | tf_op jit(solution)/shard_map/ppermute | solution.py:20
  27.4 39.0 %copy-start.2 = (s32[1,256,128]{2,1,0:T(8,128)S(1)}, s32[1,256,128]{2,1,0:T(8,128)}, u32[]{:S(2)}) copy-start(s32[1,256,128]{2,1,0:T(8,128)} %param.14) | copy-start | bytes 393220
  27.4 39.0 %copy-start.3 = (s32[1,256,128]{2,1,0:T(8,128)S(1)}, s32[1,256,128]{2,1,0:T(8,128)}, u32[]{:S(2)}) copy-start(s32[1,256,128]{2,1,0:T(8,128)} %param.13) | copy-start | bytes 393220
  39.6 20.7 %all-to-all-start.1 = ((bf16[128,5,2,128]{3,2,1,0:T(2,128)(2,1)}), bf16[128,5,2,128]{3,2,1,0:T(2,128)(2,1)}, u32[]{:S(2)}, u32[]{:S(2)}) async-start(bf16[128,5,2,128]{3,2,1,0:T(2,128)(2,1)} %pick.1), calls=%async_computation.1 | async-start | bytes 655360 | tf_op jit(solution)/shard_map/all_to_all | solution.py:399
  47.6 6.4 %collective-permute-start.4 = (f32[3,8,256]{2,1,0:T(8,128)S(1)}, f32[3,8,256]{2,1,0:T(8,128)S(1)}, u32[]{:S(2)}, u32[]{:S(2)}) collective-permute-start(f32[3,8,256]{2,1,0:T(8,128)S(1)} %get-tuple-element.44), channel_id=1, source_target_pairs={{0,8},{8,16},{16,24},{24,32},{32,40},{40,48},{48,56},{56,64},{64,7... | collective-permute-start | bytes 73736 | tf_op jit(solution)/shard_map/ppermute | solution.py:25
  48.1 6.0 %collective-permute-start.5 = (f32[3,8,256]{2,1,0:T(8,128)S(1)}, f32[3,8,256]{2,1,0:T(8,128)S(1)}, u32[]{:S(2)}, u32[]{:S(2)}) collective-permute-start(f32[3,8,256]{2,1,0:T(8,128)S(1)} %get-tuple-element.45), channel_id=1, source_target_pairs={{0,120},{8,0},{16,8},{24,16},{32,24},{40,32},{48,40},{56,48},{64,5... | collective-permute-start | bytes 73736 | tf_op jit(solution)/shard_map/ppermute | solution.py:25
  61.4 5.0 %collective-permute-start.6 = (bf16[128,1280]{1,0:T(8,128)(2,1)S(1)}, bf16[128,1280]{1,0:T(8,128)(2,1)S(1)}, u32[]{:S(2)}, u32[]{:S(2)}) collective-permute-start(bf16[128,1280]{1,0:T(8,128)(2,1)S(1)} %reshape.71.near_ref), channel_id=1, source_target_pairs={{0,128},{128,0},{1,129},{129,1},{2,130},{130,2},{3,131},{131,3},{4... | collective-permute-start | bytes 983048 | tf_op jit(solution)/shard_map/ppermute | solution.py:20
  66.4 2.2 %copy-start = (bf16[1,64,256,128]{3,2,1,0:T(8,128)(2,1)S(1)}, bf16[1,64,256,128]{3,2,1,0:T(8,128)(2,1)}, u32[]{:S(2)}) copy-start(bf16[1,64,256,128]{3,2,1,0:T(8,128)(2,1)} %param.10) | copy-start | bytes 12582916
  68.6 16.1 %copy-start.1 = (bf16[1,64,256,128]{3,2,1,0:T(8,128)(2,1)S(1)}, bf16[1,64,256,128]{3,2,1,0:T(8,128)(2,1)}, u32[]{:S(2)}) copy-start(bf16[1,64,256,128]{3,2,1,0:T(8,128)(2,1)} %param.10) | copy-start | bytes 12582916
  73.4 3.9 %collective-permute-start.7 = (f32[8,256]{1,0:T(8,128)S(1)}, f32[8,256]{1,0:T(8,128)S(1)}, u32[]{:S(2)}, u32[]{:S(2)}) collective-permute-start(f32[8,256]{1,0:T(8,128)S(1)} %get-tuple-element.35), channel_id=1, source_target_pairs={{0,1},{1,2},{2,3},{3,4},{4,5},{5,6},{6,7},{7,0},{8,9},{9,10},{10,1... | collective-permute-start | bytes 24584 | tf_op jit(solution)/shard_map/ppermute | solution.py:25
  73.8 3.4 %collective-permute-start.8 = (f32[8,256]{1,0:T(8,128)S(1)}, f32[8,256]{1,0:T(8,128)S(1)}, u32[]{:S(2)}, u32[]{:S(2)}) collective-permute-start(f32[8,256]{1,0:T(8,128)S(1)} %get-tuple-element.36), channel_id=1, source_target_pairs={{0,7},{1,0},{2,1},{3,2},{4,3},{5,4},{6,5},{7,6},{8,15},{9,8},{10,9... | collective-permute-start | bytes 24584 | tf_op jit(solution)/shard_map/ppermute | solution.py:25
  77.6 5.9 %collective-permute-start.9 = (f32[8,256]{1,0:T(8,128)S(1)}, f32[8,256]{1,0:T(8,128)S(1)}, u32[]{:S(2)}, u32[]{:S(2)}) collective-permute-start(f32[8,256]{1,0:T(8,128)S(1)} %get-tuple-element.38), channel_id=1, source_target_pairs={{0,8},{8,16},{16,24},{24,32},{32,40},{40,48},{48,56},{56,64},{64,7... | collective-permute-start | bytes 24584 | tf_op jit(solution)/shard_map/ppermute | solution.py:25
  77.7 5.8 %collective-permute-start.10 = (f32[8,256]{1,0:T(8,128)S(1)}, f32[8,256]{1,0:T(8,128)S(1)}, u32[]{:S(2)}, u32[]{:S(2)}) collective-permute-start(f32[8,256]{1,0:T(8,128)S(1)} %get-tuple-element.39), channel_id=1, source_target_pairs={{0,120},{8,0},{16,8},{24,16},{32,24},{40,32},{48,40},{56,48},{64,5... | collective-permute-start | bytes 24584 | tf_op jit(solution)/shard_map/ppermute | solution.py:25
  88.5 3.9 %collective-permute-start.11 = (f32[128,3,128]{2,1,0:T(4,128)S(1)}, f32[128,3,128]{2,1,0:T(4,128)S(1)}, u32[]{:S(2)}, u32[]{:S(2)}) collective-permute-start(f32[128,3,128]{2,1,0:T(4,128)S(1)} %pad_maximum_fusion.2), channel_id=1, source_target_pairs={{0,128},{128,0},{1,129},{129,1},{2,130},{130,2},{3,131},{131,3},{4... | collective-permute-start | bytes 589832 | tf_op jit(solution)/shard_map/ppermute | solution.py:20
  120.6 2.8 %collective-permute-start.12 = (f32[24,256]{1,0:T(8,128)S(1)}, f32[24,256]{1,0:T(8,128)S(1)}, u32[]{:S(2)}, u32[]{:S(2)}) collective-permute-start(f32[24,256]{1,0:T(8,128)S(1)} %scatter.1), channel_id=1, source_target_pairs={{0,128},{128,0},{1,129},{129,1},{2,130},{130,2},{3,131},{131,3},{4... | collective-permute-start | bytes 73736 | tf_op jit(solution)/shard_map/ppermute | solution.py:20

commit v3 on v2

--- a/solution.py
+++ b/solution.py
@@ -4,6 +4,7 @@
 from jax.experimental import pallas as pl
 from jax.experimental.pallas import tpu as pltpu
 from jax.sharding import PartitionSpec as P
+
 
 STEPS = 4
 SMB_RATE = 0.5
@@ -13,20 +14,27 @@
 F32 = jnp.float32
 BF16 = jnp.bfloat16
 EXACT = lax.Precision.HIGHEST
+COST = pl.CostEstimate(flops=0, transcendentals=0, bytes_accessed=12 << 20)
 ROOM = pltpu.CompilerParams(vmem_limit_bytes=16 << 20)
+ON_CHIP = pl.BlockSpec(memory_space=pltpu.VMEM)
+SCALARS = pl.BlockSpec(memory_space=pltpu.SMEM)
 
 
 def swap_cores(value):
     return lax.ppermute(value, "grp", [(0, 1), (1, 0)])
 
 
-def ring(value, axis, step):
+def trade(value, axis, phase):
     count = lax.axis_size(axis)
-    return lax.ppermute(value, axis, [(i, (i + step) % count) for i in range(count)])
-
-
-def after(value, *others):
-    return lax.optimization_barrier((value,) + others)[0]
+    pairs = []
+    for i in range(count):
+        other = i + 1 if i % 2 == phase else i - 1
+        pairs.append((i, other if 0 <= other < count else i))
+    return lax.ppermute(value, axis, pairs)
+
+
+def trade_both(first, second, axis):
+    return trade(first, axis, 0), trade(second, axis, 1)
 
 
 def ones_where(mask):
@@ -68,6 +76,7 @@
             jax.ShapeDtypeStruct((4 * groups, row_count), BF16),
         ),
         compiler_params=ROOM,
+        cost_estimate=COST,
         name="head",
     )(owner_row, rows)
 
@@ -117,6 +126,7 @@
         pick_kernel,
         out_shape=jax.ShapeDtypeStruct((asked.shape[0], classes // 2, 2, 128), BF16),
         compiler_params=ROOM,
+        cost_estimate=COST,
         name="pick",
     )(table, asked)
 
@@ -137,7 +147,7 @@
             row = block[s : s + 1, :]
             hot.append(hot_low(row & (LOW - 1), tiles))
             mine = high_iota == row // LOW
-            values = value_ref[start + s]
+            values = value_ref[pl.ds(3 * start + 3 * s, 3), :]
             first = values.astype(BF16).astype(F32)
             rows = []
             for part in (first, values - first):
@@ -162,6 +172,7 @@
         scatter_kernel,
         out_shape=jax.ShapeDtypeStruct((3 * high_count, LOW), F32),
         compiler_params=ROOM,
+        cost_estimate=COST,
         name="scatter",
     )(asked, values)
 
@@ -185,12 +196,27 @@
     )
 
 
-def remap_kernel(
-    near_ref, far_ref, place_ref, order_ref, weight_ref, class_ref, mask_ref,
-    source_ref, total_ref, left_ref, right_ref, table_ref,
-):
-    width, row_count, cols = weight_ref.shape
+def cut_edges(odd_ref, plane, even_ref, other_ref):
+    cols = plane.shape[1]
+    lane = lax.broadcasted_iota(jnp.int32, (EDGE, cols), 1)
+    line = lax.broadcasted_iota(jnp.int32, (EDGE, cols), 0)
+    odd = odd_ref[0] == 1
+    for out_ref, offset in (
+        (even_ref, jnp.where(odd, 0, cols - EDGE)),
+        (other_ref, jnp.where(odd, cols - EDGE, 0)),
+    ):
+        out_ref[...] = lax.dot_general(
+            jnp.where(lane == line + offset, 1.0, 0.0),
+            plane,
+            (((1,), (1,)), ((), ())),
+            precision=EXACT,
+            preferred_element_type=F32,
+        )
+
+
+def table_kernel(near_ref, far_ref, place_ref, order_ref, table_ref):
     groups = near_ref.shape[0]
+    row_count = table_ref.shape[0]
     classes = near_ref.shape[1] // 128
 
     answers = jnp.concatenate([near_ref[...], far_ref[...]], axis=0)
@@ -222,6 +248,11 @@
         jnp.concatenate(picked, axis=1), order_ref[...], preferred_element_type=F32
     ).astype(BF16)
 
+
+def remap_kernel(
+    odd_ref, table_ref, weight_ref, class_ref, mask_ref, source_ref, total_ref, even_ref, other_ref
+):
+    width, row_count, cols = weight_ref.shape
     tile = min(32, row_count)
 
     def remap_rows(i, carry):
@@ -243,84 +274,107 @@
         return carry
 
     lax.fori_loop(0, row_count // tile, remap_rows, 0)
-
-    lane = lax.broadcasted_iota(jnp.int32, (EDGE, cols), 1)
-    line = lax.broadcasted_iota(jnp.int32, (EDGE, cols), 0)
-    for out_ref, offset in ((left_ref, 0), (right_ref, cols - EDGE)):
-        out_ref[...] = lax.dot_general(
-            jnp.where(lane == line + offset, 1.0, 0.0),
-            source_ref[...],
-            (((1,), (1,)), ((), ())),
-            precision=EXACT,
-            preferred_element_type=F32,
-        )
-
-
-def remap(near, far, place, order, weights, classes, mask):
+    cut_edges(odd_ref, source_ref[...], even_ref, other_ref)
+
+
+def remap(odd, near, far, place, order, weights, classes, mask):
     row_count, cols = weights.shape[1:]
+    table = pl.pallas_call(
+        table_kernel,
+        in_specs=[ON_CHIP] * 4,
+        out_specs=ON_CHIP,
+        out_shape=jax.ShapeDtypeStruct((row_count, order.shape[1]), BF16),
+        compiler_params=ROOM,
+        cost_estimate=COST,
+        name="table",
+    )(near, far, place, order)
+    edge = jax.ShapeDtypeStruct((EDGE, row_count), F32)
     plane = jax.ShapeDtypeStruct((row_count, cols), F32)
-    edge = jax.ShapeDtypeStruct((EDGE, row_count), F32)
     return pl.pallas_call(
         remap_kernel,
+        in_specs=[SCALARS] + [ON_CHIP] * 4,
+        out_specs=[ON_CHIP] * 4,
         out_shape=(plane, plane, edge, edge),
-        scratch_shapes=[pltpu.VMEM((row_count, order.shape[1]), BF16)],
-        compiler_params=ROOM,
+        compiler_params=ROOM,
+        cost_estimate=COST,
         name="remap",
-    )(near, far, place, order, weights, classes, mask)
-
-
-def side_kernel(source_ref, low_ref, high_ref, side_ref, top_ref, bottom_ref):
+    )(odd, table, weights, classes, mask)
+
+
+def side_kernel(
+    odd_ref, source_ref, bed_ref, diff_ref, thick_ref, even_ref, other_ref, fixed_even_ref,
+    fixed_other_ref, side_ref, send_ref, send_other_ref,
+):
     row_count, cols = source_ref.shape
     lane = lax.broadcasted_iota(jnp.int32, (2 * EDGE, cols), 1)
     line = lax.broadcasted_iota(jnp.int32, (2 * EDGE, cols), 0)
+    line = jnp.where(odd_ref[0] == 1, (line + EDGE) % (2 * EDGE), line)
     spot = jnp.where(line < EDGE, line, line + cols - 2 * EDGE)
-    side = lax.dot_general(
-        jnp.concatenate([high_ref[...], low_ref[...]], axis=0),
-        jnp.where(lane == spot, 1.0, 0.0),
-        (((0,), (0,)), ((), ())),
-        precision=EXACT,
-        preferred_element_type=F32,
-    )
-    side_ref[...] = side
-    for out_ref, first in ((top_ref, 0), (bottom_ref, row_count - EDGE)):
-        out_ref[:, :cols] = source_ref[first : first + EDGE, :]
-        out_ref[:, cols:] = side[first : first + EDGE, :]
-
-
-def side(source, from_low, from_high):
+    spread = jnp.where(lane == spot, 1.0, 0.0)
+    odd = odd_ref[1] == 1
+    for p, plane_ref in enumerate((source_ref, bed_ref, diff_ref, thick_ref)):
+        if p == 0:
+            edges = [even_ref[...], other_ref[...]]
+        else:
+            edges = [fixed_even_ref[p - 1], fixed_other_ref[p - 1]]
+        side = lax.dot_general(
+            jnp.concatenate(edges, axis=0),
+            spread,
+            (((0,), (0,)), ((), ())),
+            precision=EXACT,
+            preferred_element_type=F32,
+        )
+        side_ref[p] = side
+        first = jnp.concatenate([plane_ref[:EDGE, :], side[:EDGE]], axis=1)
+        last = jnp.concatenate(
+            [plane_ref[row_count - EDGE :, :], side[row_count - EDGE :]], axis=1
+        )
+        send_ref[p] = jnp.where(odd, first, last)
+        send_other_ref[p] = jnp.where(odd, last, first)
+
+
+def side(odd, source, bed, diff, thick, edges, fixed_edges):
     row_count, cols = source.shape
+    strip = jax.ShapeDtypeStruct((4, EDGE, 2 * cols), F32)
     return pl.pallas_call(
         side_kernel,
-        out_shape=(
-            jax.ShapeDtypeStruct((row_count, cols), F32),
-            jax.ShapeDtypeStruct((EDGE, 2 * cols), F32),
-            jax.ShapeDtypeStruct((EDGE, 2 * cols), F32),
-        ),
-        compiler_params=ROOM,
+        in_specs=[SCALARS] + [ON_CHIP] * 8,
+        out_specs=[ON_CHIP] * 3,
+        out_shape=(jax.ShapeDtypeStruct((4, row_count, cols), F32), strip, strip),
+        compiler_params=ROOM,
+        cost_estimate=COST,
         name="side",
-    )(source, from_low, from_high)
+    )(odd, source, bed, diff, thick, *edges, *fixed_edges)
 
 
 def relax_kernel(
-    source_ref, side_ref, above_ref, below_ref, fixed_ref, inside_ref, total_ref, mask_ref,
-    thick_ref, field_ref,
+    odd_ref, source_ref, bed_ref, diff_ref, start_ref, side_ref, even_ref, other_ref,
+    inside_ref, total_ref, mask_ref, thick_ref, field_ref,
 ):
     row_count, cols = source_ref.shape
     rows, lanes = inside_ref.shape
     ahead = lambda a, axis: pltpu.roll(a, (rows, lanes)[axis] - 1, axis)
     back = lambda a, axis: pltpu.roll(a, 1, axis)
-    source = SMB_RATE * jnp.concatenate(
-        [
-            above_ref[...],
-            jnp.concatenate([source_ref[...], side_ref[...]], axis=1),
-            below_ref[...],
-        ],
-        axis=0,
-    )
-    bed, diff, thick = fixed_ref[0], fixed_ref[1], fixed_ref[2]
     inside = inside_ref[...]
+    odd = odd_ref[1] == 1
+    planes = []
+    for p, plane_ref in enumerate((source_ref, bed_ref, diff_ref, start_ref)):
+        even, other = even_ref[p], other_ref[p]
+        planes.append(
+            inside
+            * jnp.concatenate(
+                [
+                    jnp.where(odd, even, other),
+                    jnp.concatenate([plane_ref[...], side_ref[p]], axis=1),
+                    jnp.where(odd, other, even),
+                ],
+                axis=0,
+            )
+        )
+    source, bed, diff, thick = planes
+    source = SMB_RATE * source
     gain = [0.5 * (diff + ahead(diff, axis)) for axis in range(2)]
-    for step in range(STEPS):
+    for _ in range(STEPS):
         surface = bed + thick
         change = source
         for axis in range(2):
@@ -330,24 +384,27 @@
     own = thick[EDGE : EDGE + row_count, :cols]
     thick_ref[...] = own
     total = total_ref[...]
-    field_ref[0] = ((bed[EDGE : EDGE + row_count, :cols] + own) / total).astype(BF16)
+    field_ref[0] = ((bed_ref[...] + own) / total).astype(BF16)
     field_ref[1] = (mask_ref[...].astype(F32) * jnp.minimum(own, 1.0) / total).astype(BF16)
     field_ref[2] = (1.0 / total).astype(BF16)
 
 
-def relax(source, side_tile, above, below, fixed, inside, total, mask):
+def relax(odd, source, bed, diff, thick, sides, strips, inside, total, mask):
     return pl.pallas_call(
         relax_kernel,
+        in_specs=[SCALARS] + [ON_CHIP] * 10,
+        out_specs=[ON_CHIP] * 2,
         out_shape=(
             jax.ShapeDtypeStruct(source.shape, F32),
             jax.ShapeDtypeStruct((3,) + source.shape, BF16),
         ),
         compiler_params=ROOM,
+        cost_estimate=COST,
         name="relax",
-    )(source, side_tile, above, below, fixed, inside, total, mask)
-
-
-def per_device(
+    )(odd, source, bed, diff, thick, sides, *strips, inside, total, mask)
+
+
+def coupled(
     fluxes, weights, land_rows, owners, elev_class, ice_mask, bed, thickness, diffusivity
 ):
     groups = lax.axis_size("gx") * lax.axis_size("gy")
@@ -363,23 +420,22 @@
     request = jnp.where(is_ice, low_half, swap_cores(high_half))
     asked = lax.all_to_all(request, PLANES, split_axis=0, concat_axis=0, tiled=True)
 
-    flux, fixed = lax.optimization_barrier(
-        (fluxes[0], jnp.stack([bed[0], diffusivity[0], thickness[0]]), request)
-    )[:2]
+    flux, bed_now, diff_now, thick_now = lax.optimization_barrier(
+        (fluxes[0], bed[0], diffusivity[0], thickness[0], request)
+    )[:4]
     table = jnp.pad(flux.astype(BF16), ((0, 16 - classes), (0, 0)))
     table = jnp.transpose(table.reshape(16, high_count, LOW), (1, 0, 2)).reshape(-1, LOW)
-    table = jnp.where(is_ice, swap_cores(table), table)
-    turn = lambda part: jnp.transpose(part, (0, 2, 1))
-    from_low = turn(ring(turn(fixed[:, :, cols - STEPS :]), "gy", 1))
-    from_high = turn(ring(turn(fixed[:, :, :STEPS]), "gy", -1))
-    fixed = jnp.concatenate(
-        [fixed, from_high, jnp.zeros((3, row_count, cols - 2 * STEPS), F32), from_low], axis=2
-    )
+    other_table = swap_cores(table)
+    table = jnp.where(is_ice, other_table, table)
+    at_x, at_y = lax.axis_index("gx"), lax.axis_index("gy")
+    odd = jnp.stack([at_y % 2, at_x % 2]).astype(jnp.int32)
+    turn = lambda cut: jnp.stack([jnp.transpose(a[:, cut]) for a in (bed_now, diff_now, thick_now)])
+    first, last = turn(slice(0, EDGE)), turn(slice(cols - EDGE, cols))
+    fixed_edges = [jnp.where(odd[0] == 1, first, last), jnp.where(odd[0] == 1, last, first)]
 
     row_at = lax.broadcasted_iota(jnp.int32, (row_count + 2 * EDGE, 2 * cols), 0) - EDGE
     col_at = lax.broadcasted_iota(jnp.int32, (row_count + 2 * EDGE, 2 * cols), 1)
     col_at = jnp.where(col_at < cols + cols // 2, col_at, col_at - 2 * cols)
-    at_x, at_y = lax.axis_index("gx"), lax.axis_index("gy")
     inside = (
         ((row_at >= 0) | (at_x > 0))
         & ((row_at < row_count) | (at_x < lax.axis_size("gx") - 1))
@@ -388,35 +444,27 @@
     ).astype(F32)
     line = lax.broadcasted_iota(jnp.int32, (classes * width, 16 * width), 0)
     lane = lax.broadcasted_iota(jnp.int32, (classes * width, 16 * width), 1)
-    order = (
-        (lane // 128 == line % width // 8)
-        & (lane % 128 // 8 == line // width)
-        & (lane % 8 == line % 8)
-    ).astype(BF16)
-
-    asked, fixed, order, inside = lax.optimization_barrier((asked, fixed, order, inside))
+    source_line = ((lane & 127) >> 3) * width + (lane >> 7) * 8 + (lane & 7)
+    order = (source_line == line).astype(BF16)
+
+    asked, order, inside, *fixed_edges = lax.optimization_barrier(
+        (asked, order, inside, *fixed_edges)
+    )
     answer = pick(table, asked, classes)
     near = lax.all_to_all(answer, PLANES, split_axis=0, concat_axis=0, tiled=True)
-
-    fixed = after(fixed, answer)
-    above = ring(fixed[:, row_count - EDGE :], "gx", 1)
-    below = ring(fixed[:, :EDGE], "gx", -1)
-    fixed = jnp.concatenate([above, fixed, below], axis=1) * inside
-    near, fixed = lax.optimization_barrier((near, fixed))
+    fixed_edges = trade_both(*fixed_edges, "gy")
+    near, *fixed_edges = lax.optimization_barrier((near, *fixed_edges))
 
     near = near.reshape(groups, classes * 128)
-    source, total, left, right = remap(
-        near, swap_cores(near), place, order, block_weights, elev_class[0], ice_mask[0]
-    )
-    side_tile, top, bottom = side(source, ring(right, "gy", 1), ring(left, "gy", -1))
+    source, total, *edges = remap(
+        odd, near, swap_cores(near), place, order, block_weights, elev_class[0], ice_mask[0]
+    )
+    sides, *strips = side(
+        odd, source, bed[0], diffusivity[0], thickness[0], trade_both(*edges, "gy"), fixed_edges
+    )
+    strips = trade_both(*strips, "gx")
     thick, fields = relax(
-        source,
-        side_tile,
-        ring(bottom, "gx", 1),
-        ring(top, "gx", -1),
-        fixed,
-        inside,
-        total,
+        odd, source, bed[0], diffusivity[0], thickness[0], sides, strips, inside, total,
         ice_mask[0],
     )
 
@@ -430,8 +478,10 @@
     )
     outgoing = [jnp.concatenate([outgoing[k], outgoing[k + 1]], axis=2) for k in (0, 2)]
     sent = jnp.where(is_ice, outgoing[0], swap_cores(outgoing[1]))
-    arrived = lax.all_to_all(sent, PLANES, split_axis=0, concat_axis=0, tiled=True)
-    land_sums = scatter(asked, arrived, high_count)
+    arrived = lax.all_to_all(
+        sent.reshape(groups, -1), PLANES, split_axis=0, concat_axis=0, tiled=True
+    )
+    land_sums = scatter(asked, arrived.reshape(3 * groups, 128), high_count)
     land_sums = (land_sums + swap_cores(land_sums)).reshape(3, cells)
     averaged = land_sums[:2] / jnp.maximum(land_sums[2], 1.0)
     land_fields = jnp.where(is_ice, 0.0, averaged)[None]
@@ -441,7 +491,7 @@
 
 def solution(mesh):
     return jax.shard_map(
-        per_device,
+        coupled,
         mesh=mesh,
         in_specs=(
             P("grp", None, ("gx", "gy")),

time: 125 us -> 118 us (0.944)
  starting transfers between devices: 47.7 us -> 35.1 us
  waiting for transfers between devices: 18.4 us -> 26.3 us
  other arithmetic: 8.37 us -> 2.64 us
  Pallas kernels: 12.2 us -> 14.2 us
  blocking collectives: 25.2 us -> 27 us
    ppermute x8 -> x6, starting transfers between devices: 16.3 us -> 3.22 us  [trade(): return lax.ppermute(value, axis, pairs)]
    ppermute x8 -> x6, waiting for transfers between devices: 3.72 us -> 8.86 us  [trade(): return lax.ppermute(value, axis, pairs)]
    another operation x0 -> x8, local copies, waits for them, and re-layouts: none -> 2.7 us  [coupled(): jnp.stack([jnp.transpose(a[:, cut]) for a in (bed_now, diff_now, thick_no...]
    all_to_all x2, waiting for transfers between devices: 12.3 us -> 14.9 us  [the longest x1 7.61 us: coupled(): lax.all_to_all(answer, PLANES, split_axis=0, concat_axis=0, tiled=True)]
    concatenate x2 -> x1, other arithmetic: 2.42 us -> 0.02 us  [coupled(): jnp.concatenate([outgoing[k], outgoing[k + 1]], axis=2)]
    pallas_call x3 -> x4, Pallas kernels: 6.31 us -> 8.27 us  [the longest x1 4.33 us: remap(): pl.pallas_call(remap_kernel, in_specs=[SCALARS] + [ON_CHIP] * 4, out_spec...]
    all_to_all x1, blocking collectives: 25.2 us -> 27 us  [coupled(): lax.all_to_all(sent.reshape(groups, -1), PLANES, split_axis=0, concat_axi...]
    all_to_all x2, starting transfers between devices: 18.6 us -> 20 us  [the longest x1 13.8 us: coupled(): lax.all_to_all(request, PLANES, split_axis=0, concat_axis=0, tiled=True)]
  transfers between devices with their start and end apart: 15 -> 13, of which waited for: 8 -> 8; matrix products, arithmetic and copies ran while one was open for 7% -> 4% of each run, Pallas kernels for 0% -> 0%
where the time goes in v3:
time: 118 us; the launch traced here: 117 us
  starting transfers between devices  35.1 us (30%)
  blocking collectives  27 us (23%)
  waiting for transfers between devices  26.3 us (22%)
  Pallas kernels  14.2 us (12%)
  local copies, waits for them, and re-layouts  7.89 us (7%)
  matrix products  3.11 us (3%)
  other arithmetic  2.64 us (2%)
    all_to_all x1, blocking collectives, coupled(): lax.all_to_all(sent.reshape(groups, -1), PLANES, split_axis=0, concat_axi...  27 us
    all_to_all x1, starting transfers between devices, coupled(): lax.all_to_all(request, PLANES, split_axis=0, concat_axis=0, tiled=True)  13.8 us
    ppermute x5, starting transfers between devices, swap_cores(): return lax.ppermute(value, 'grp', [(0, 1), (1, 0)])  11.9 us
    ppermute x6, waiting for transfers between devices, trade(): return lax.ppermute(value, axis, pairs)  8.86 us
    all_to_all x1, waiting for transfers between devices, coupled(): lax.all_to_all(answer, PLANES, split_axis=0, concat_axis=0, tiled=True)  7.61 us
    all_to_all x1, waiting for transfers between devices, coupled(): lax.all_to_all(request, PLANES, split_axis=0, concat_axis=0, tiled=True)  7.33 us
    all_to_all x1, starting transfers between devices, coupled(): lax.all_to_all(answer, PLANES, split_axis=0, concat_axis=0, tiled=True)  6.21 us
    unnamed x20, local copies, waits for them, and re-layouts  4.65 us
  transfers between devices with their start and end apart: 13, of which 8 were waited for; matrix products, arithmetic and copies ran while one was open for 4% of the time, Pallas kernels for 0%

profile of v3, /device:TPU:1, one launch (start us, length us, event | category | flops | bytes accessed | tf_op | source)
XLA Modules:
  0.0 117.1 jit_solution(5275479774668376372)
XLA Ops:
  0.6 0.8 copy-done.7
  1.5 0.7 copy-done.8
  2.7 3.3 %collective-permute-start = (s32[128,128]{1,0:T(8,128)S(1)}, s32[128,128]{1,0:T(8,128)S(1)}, u32[]{:S(2)}, u32[]{:S(2)}) collective-permute-start(s32[128,128]{1,0:T(8,128)S(1)} %get-tuple-element.27), channel_id=1, source_target_pairs={{0,128},{128,0},{1,129},{129,1},{2,130},{130,2},{3,131},{131,3},{4... | collective-permute-start | bytes 196616 | tf_op jit(solution)/shard_map/ppermute | solution.py:24
  6.6 0.9 copy.37
  8.2 13.8 %all-to-all-start = ((s32[128,1,128]{2,1,0:T(1,128)}), s32[128,1,128]{2,1,0:T(1,128)S(1)}, u32[]{:S(2)}, u32[]{:S(2)}) async-start(s32[128,1,128]{2,1,0:T(1,128)} %bitcast.4), calls=%async_computation | async-start | bytes 131072 | tf_op jit(solution)/shard_map/all_to_all | solution.py:421
  22.4 1.1 slice_bitcast_fusion.5
  23.6 1.2 %slice_bitcast_fusion.3 = (f32[1,8,256]{1,2,0:T(8,128)S(1)}, f32[1,8,256]{1,2,0:T(8,128)S(1)}, f32[1,8,256]{1,2,0:T(8,128)S(1)}, f32[1,8,256]{1,2,0:T(8,128)S(1)}) fusion(f32[256,128]{1,0:T(8,128)} %bitcast.85, f32[256,128]{1,0:T(8,128)} %bitcast.82), kind=kLoop, calls=%fused_computation.22 | loop fusion | bytes 65536 | tf_op jit(solution)/shard_map/stack | solution.py:432
  25.2 7.3 %all-to-all-done = s32[128,1,128]{2,1,0:T(1,128)S(1)} async-done(((s32[128,1,128]{2,1,0:T(1,128)}), s32[128,1,128]{2,1,0:T(1,128)S(1)}, u32[]{:S(2)}, u32[]{:S(2)}) %all-to-all-start) | async-done | bytes 65568 | tf_op jit(solution)/shard_map/all_to_all | solution.py:421
  32.5 2.6 %pick.1 = bf16[128,5,2,128]{3,2,1,0:T(2,128)(2,1)} custom-call(bf16[128,256]{1,0:T(8,128)(2,1)S(1)} %broadcast_select_fusion.table_ref, s32[128,128]{1,0:T(8,128)S(1)} %bitcast.90), custom_call_target="tpu_custom_call" | custom-call | bytes 12582912 | tf_op jit(solution)/shard_map/pick/pallas_call | solution.py:125
  35.1 6.2 %all-to-all-start.1 = ((bf16[128,5,2,128]{3,2,1,0:T(2,128)(2,1)}), bf16[128,5,2,128]{3,2,1,0:T(2,128)(2,1)S(1)}, u32[]{:S(2)}, u32[]{:S(2)}) async-start(bf16[128,5,2,128]{3,2,1,0:T(2,128)(2,1)} %pick.1), calls=%async_computation.1 | async-start | bytes 655360 | tf_op jit(solution)/shard_map/all_to_all | solution.py:454
  41.4 0.7 collective-permute-start.2
  42.1 0.7 collective-permute-start.3
  42.7 5.4 %collective-permute-done.2.fixed_even_ref = f32[3,8,256]{2,1,0:T(8,128)S(1)} collective-permute-done((f32[3,8,256]{2,1,0:T(8,128)S(1)}, f32[3,8,256]{2,1,0:T(8,128)S(1)}, u32[]{:S(2)}, u32[]{:S(2)}) %collective-permute-start.2) | collective-permute-done | bytes 24608 | tf_op jit(solution)/shard_map/ppermute | solution.py:33
  48.1 7.6 %all-to-all-done.1 = bf16[128,5,2,128]{3,2,1,0:T(2,128)(2,1)S(1)} async-done(((bf16[128,5,2,128]{3,2,1,0:T(2,128)(2,1)}), bf16[128,5,2,128]{3,2,1,0:T(2,128)(2,1)S(1)}, u32[]{:S(2)}, u32[]{:S(2)}) %all-to-all-start.1) | async-done | bytes 327712 | tf_op jit(solution)/shard_map/all_to_all | solution.py:454
  55.9 3.4 %collective-permute-start.4 = (bf16[128,1280]{1,0:T(8,128)(2,1)S(1)}, bf16[128,1280]{1,0:T(8,128)(2,1)S(1)}, u32[]{:S(2)}, u32[]{:S(2)}) collective-permute-start(bf16[128,1280]{1,0:T(8,128)(2,1)S(1)} %reshape.78.near_ref), channel_id=1, source_target_pairs={{0,128},{128,0},{1,129},{129,1},{2,130},{130,2},{3,131},{131,3},{4... | collective-permute-start | bytes 983048 | tf_op jit(solution)/shard_map/ppermute | solution.py:24
  59.4 1.2 %collective-permute-done.4.far_ref = bf16[128,1280]{1,0:T(8,128)(2,1)S(1)} collective-permute-done((bf16[128,1280]{1,0:T(8,128)(2,1)S(1)}, bf16[128,1280]{1,0:T(8,128)(2,1)S(1)}, u32[]{:S(2)}, u32[]{:S(2)}) %collective-permute-start.4) | collective-permute-done | bytes 327712 | tf_op jit(solution)/shard_map/ppermute | solution.py:24
  60.5 1.0 table.1.table_ref
  61.6 2.2 %copy-done = bf16[1,64,256,128]{3,2,1,0:T(8,128)(2,1)S(1)} copy-done((bf16[1,64,256,128]{3,2,1,0:T(8,128)(2,1)S(1)}, bf16[1,64,256,128]{3,2,1,0:T(8,128)(2,1)}, u32[]{:S(2)}) %copy-start) | copy-done | bytes 4194328
  63.8 4.3 %remap.1 = (f32[256,128]{1,0:T(8,128)S(1)}, f32[256,128]{1,0:T(8,128)S(1)}, f32[8,256]{1,0:T(8,128)S(1)}, f32[8,256]{1,0:T(8,128)S(1)}) custom-call(s32[2]{0:T(128)S(1)} %pad_add_fusion.odd_ref, bf16[256,1024]{1,0:T(8,128)(2,1)S(1)} %table.1.table_ref, bf16[64,256,128]{2,1,0:T(8,128)(2,1)S(1)} %bitcast.77, s32[256,128]{1,0:T(8,128)S(1)} %bitcast.94, ...), custom_call_target="tpu_custom_call" | custom-call | bytes 12582912 | tf_op jit(solution)/shard_map/remap/pallas_call | solution.py:293
  68.4 0.6 collective-permute-start.6
  69.1 1.5 %collective-permute-done.5.even_ref = f32[8,256]{1,0:T(8,128)S(1)} collective-permute-done((f32[8,256]{1,0:T(8,128)S(1)}, f32[8,256]{1,0:T(8,128)S(1)}, u32[]{:S(2)}, u32[]{:S(2)}) %collective-permute-start.5) | collective-permute-done | bytes 8224 | tf_op jit(solution)/shard_map/ppermute | solution.py:33
  70.7 1.2 %side.1 = (f32[4,256,128]{2,1,0:T(8,128)S(1)}, f32[4,8,256]{2,1,0:T(8,128)S(1)}, f32[4,8,256]{2,1,0:T(8,128)S(1)}) custom-call(s32[2]{0:T(128)S(1)} %pad_add_fusion.odd_ref, f32[256,128]{1,0:T(8,128)S(1)} %get-tuple-element.38.source_ref, f32[256,128]{1,0:T(8,128)S(1)} %bitcast.80, f32[256,128]{1,0:T(8,128)S(1)} %bitcast.83, f32[256,128]{1,0:T(8,128)S(1)} %bitcast.86, ...), custom_call_target="tpu_custom_call" | custom-call | bytes 12582912 | tf_op jit(solution)/shard_map/side/pallas_call | solution.py:339
  72.0 0.8 collective-permute-start.8
  72.8 1.9 %collective-permute-done.7.even_ref = f32[4,8,256]{2,1,0:T(8,128)S(1)} collective-permute-done((f32[4,8,256]{2,1,0:T(8,128)S(1)}, f32[4,8,256]{2,1,0:T(8,128)S(1)}, u32[]{:S(2)}, u32[]{:S(2)}) %collective-permute-start.7) | collective-permute-done | bytes 32800 | tf_op jit(solution)/shard_map/ppermute | solution.py:33
  74.7 1.7 %relax.1 = (f32[256,128]{1,0:T(8,128)S(1)}, bf16[3,256,128]{2,1,0:T(8,128)(2,1)S(1)}) custom-call(s32[2]{0:T(128)S(1)} %pad_add_fusion.odd_ref, f32[256,128]{1,0:T(8,128)S(1)} %get-tuple-element.38.source_ref, f32[256,128]{1,0:T(8,128)S(1)} %bitcast.81, f32[256,128]{1,0:T(8,128)S(1)} %bitcast.84, f32[256,128]{1,0:T(8,128)S(1)} %bitcast.87, ...), custom_call_target="tpu_custom_call" | custom-call | bytes 12582912 | tf_op jit(solution)/shard_map/relax/pallas_call | solution.py:393
  76.5 2.7 %fusion = f32[256,3,64]{2,1,0:T(4,128)S(1)} fusion(bf16[64,256,128]{2,1,0:T(8,128)(2,1)S(1)} %bitcast.78, bf16[3,256,128]{2,1,0:T(8,128)(2,1)S(1)} %get-tuple-element.48), kind=kOutput, calls=%fused_computation | convolution fusion | flops 12582912 | bytes 4587520 | tf_op jit(solution)/shard_map/brj,qrj->qrb/dot_general | solution.py:471
  79.8 2.8 %collective-permute-start.9 = (f32[128,3,128]{0,2,1:T(8,128)S(1)}, f32[128,3,128]{0,2,1:T(8,128)S(1)}, u32[]{:S(2)}, u32[]{:S(2)}) collective-permute-start(f32[128,3,128]{0,2,1:T(8,128)S(1)} %pad_maximum_fusion), channel_id=1, source_target_pairs={{0,128},{128,0},{1,129},{129,1},{2,130},{130,2},{3,131},{131,3},{4... | collective-permute-start | bytes 589832 | tf_op jit(solution)/shard_map/ppermute | solution.py:24
  82.6 1.1 collective-permute-done.9
  83.8 27.0 %all_to_all.26 = f32[128,1,384]{2,1,0:T(1,128)S(1)} all-to-all(f32[128,1,384]{2,1,0:T(1,128)S(1)} %copy.23), channel_id=1, replica_groups=mesh['grp'=2,'gx'=16,'gy'=8] {'gx','gy'}, dimensions={0} | all-to-all | bytes 393216 | tf_op jit(solution)/shard_map/all_to_all | solution.py:481
  110.8 2.8 %scatter.1 = f32[24,256]{1,0:T(8,128)S(1)} custom-call(s32[128,128]{1,0:T(8,128)S(1)} %bitcast.91, f32[384,128]{1,0:T(8,128)S(1)} %bitcast.89), custom_call_target="tpu_custom_call" | custom-call | bytes 12582912 | tf_op jit(solution)/shard_map/scatter/pallas_call | solution.py:171
  113.6 2.0 %collective-permute-start.10 = (f32[24,256]{1,0:T(8,128)S(1)}, f32[24,256]{1,0:T(8,128)S(1)}, u32[]{:S(2)}, u32[]{:S(2)}) collective-permute-start(f32[24,256]{1,0:T(8,128)S(1)} %scatter.1), channel_id=1, source_target_pairs={{0,128},{128,0},{1,129},{129,1},{2,130},{130,2},{3,131},{131,3},{4... | collective-permute-start | bytes 73736 | tf_op jit(solution)/shard_map/ppermute | solution.py:24
  115.6 0.7 select_bitcast_fusion
  (56 shorter events, 4.9 us)
Async XLA Ops:
  0.6 0.8 copy-start.7
  1.5 0.7 copy-start.8
  2.7 4.8 %collective-permute-start = (s32[128,128]{1,0:T(8,128)S(1)}, s32[128,128]{1,0:T(8,128)S(1)}, u32[]{:S(2)}, u32[]{:S(2)}) collective-permute-start(s32[128,128]{1,0:T(8,128)S(1)} %get-tuple-element.27), channel_id=1, source_target_pairs={{0,128},{128,0},{1,129},{129,1},{2,130},{130,2},{3,131},{131,3},{4... | collective-permute-start | bytes 196616 | tf_op jit(solution)/shard_map/ppermute | solution.py:24
  6.4 55.1 %copy-start.5 = (s32[1,256,128]{2,1,0:T(8,128)S(1)}, s32[1,256,128]{2,1,0:T(8,128)}, u32[]{:S(2)}) copy-start(s32[1,256,128]{2,1,0:T(8,128)} %param.14) | copy-start | bytes 393220
  6.4 55.1 %copy-start.6 = (s32[1,256,128]{2,1,0:T(8,128)S(1)}, s32[1,256,128]{2,1,0:T(8,128)}, u32[]{:S(2)}) copy-start(s32[1,256,128]{2,1,0:T(8,128)} %param.13) | copy-start | bytes 393220
  8.2 24.3 %all-to-all-start = ((s32[128,1,128]{2,1,0:T(1,128)}), s32[128,1,128]{2,1,0:T(1,128)S(1)}, u32[]{:S(2)}, u32[]{:S(2)}) async-start(s32[128,1,128]{2,1,0:T(1,128)} %bitcast.4), calls=%async_computation | async-start | bytes 131072 | tf_op jit(solution)/shard_map/all_to_all | solution.py:421
  22.0 3.1 %collective-permute-start.1 = (bf16[128,256]{1,0:T(8,128)(2,1)S(1)}, bf16[128,256]{1,0:T(8,128)(2,1)S(1)}, u32[]{:S(2)}, u32[]{:S(2)}) collective-permute-start(bf16[128,256]{1,0:T(8,128)(2,1)S(1)} %bitcast.98), channel_id=1, source_target_pairs={{0,128},{128,0},{1,129},{129,1},{2,130},{130,2},{3,131},{131,3},{4... | collective-permute-start | bytes 196616 | tf_op jit(solution)/shard_map/ppermute | solution.py:24
  35.1 20.6 %all-to-all-start.1 = ((bf16[128,5,2,128]{3,2,1,0:T(2,128)(2,1)}), bf16[128,5,2,128]{3,2,1,0:T(2,128)(2,1)S(1)}, u32[]{:S(2)}, u32[]{:S(2)}) async-start(bf16[128,5,2,128]{3,2,1,0:T(2,128)(2,1)} %pick.1), calls=%async_computation.1 | async-start | bytes 655360 | tf_op jit(solution)/shard_map/all_to_all | solution.py:454
  41.4 29.3 %copy-start.2 = (f32[1,256,128]{2,1,0:T(8,128)S(1)}, f32[1,256,128]{2,1,0:T(8,128)}, u32[]{:S(2)}) copy-start(f32[1,256,128]{2,1,0:T(8,128)} %param.15) | copy-start | bytes 393220
  41.4 29.3 %copy-start.3 = (f32[1,256,128]{2,1,0:T(8,128)S(1)}, f32[1,256,128]{2,1,0:T(8,128)}, u32[]{:S(2)}) copy-start(f32[1,256,128]{2,1,0:T(8,128)} %param.17) | copy-start | bytes 393220
  41.4 29.3 %copy-start.4 = (f32[1,256,128]{2,1,0:T(8,128)S(1)}, f32[1,256,128]{2,1,0:T(8,128)}, u32[]{:S(2)}) copy-start(f32[1,256,128]{2,1,0:T(8,128)} %param.16) | copy-start | bytes 393220
  41.4 6.7 %collective-permute-start.2 = (f32[3,8,256]{2,1,0:T(8,128)S(1)}, f32[3,8,256]{2,1,0:T(8,128)S(1)}, u32[]{:S(2)}, u32[]{:S(2)}) collective-permute-start(f32[3,8,256]{2,1,0:T(8,128)S(1)} %get-tuple-element.34), channel_id=1, source_target_pairs={{0,1},{1,0},{2,3},{3,2},{4,5},{5,4},{6,7},{7,6},{8,9},{9,8},{10,11... | collective-permute-start | bytes 73736 | tf_op jit(solution)/shard_map/ppermute | solution.py:33
  42.1 6.1 %collective-permute-start.3 = (f32[3,8,256]{2,1,0:T(8,128)S(1)}, f32[3,8,256]{2,1,0:T(8,128)S(1)}, u32[]{:S(2)}, u32[]{:S(2)}) collective-permute-start(f32[3,8,256]{2,1,0:T(8,128)S(1)} %get-tuple-element.35), channel_id=1, source_target_pairs={{0,0},{1,2},{2,1},{3,4},{4,3},{5,6},{6,5},{7,7},{8,8},{9,10},{10,9... | collective-permute-start | bytes 73736 | tf_op jit(solution)/shard_map/ppermute | solution.py:33
  55.9 4.7 %collective-permute-start.4 = (bf16[128,1280]{1,0:T(8,128)(2,1)S(1)}, bf16[128,1280]{1,0:T(8,128)(2,1)S(1)}, u32[]{:S(2)}, u32[]{:S(2)}) collective-permute-start(bf16[128,1280]{1,0:T(8,128)(2,1)S(1)} %reshape.78.near_ref), channel_id=1, source_target_pairs={{0,128},{128,0},{1,129},{129,1},{2,130},{130,2},{3,131},{131,3},{4... | collective-permute-start | bytes 983048 | tf_op jit(solution)/shard_map/ppermute | solution.py:24
  61.6 2.2 %copy-start = (bf16[1,64,256,128]{3,2,1,0:T(8,128)(2,1)S(1)}, bf16[1,64,256,128]{3,2,1,0:T(8,128)(2,1)}, u32[]{:S(2)}) copy-start(bf16[1,64,256,128]{3,2,1,0:T(8,128)(2,1)} %param.10) | copy-start | bytes 12582916
  63.8 12.7 %copy-start.1 = (bf16[1,64,256,128]{3,2,1,0:T(8,128)(2,1)S(1)}, bf16[1,64,256,128]{3,2,1,0:T(8,128)(2,1)}, u32[]{:S(2)}) copy-start(bf16[1,64,256,128]{3,2,1,0:T(8,128)(2,1)} %param.10) | copy-start | bytes 12582916
  68.1 2.5 %collective-permute-start.5 = (f32[8,256]{1,0:T(8,128)S(1)}, f32[8,256]{1,0:T(8,128)S(1)}, u32[]{:S(2)}, u32[]{:S(2)}) collective-permute-start(f32[8,256]{1,0:T(8,128)S(1)} %get-tuple-element.39), channel_id=1, source_target_pairs={{0,1},{1,0},{2,3},{3,2},{4,5},{5,4},{6,7},{7,6},{8,9},{9,8},{10,11... | collective-permute-start | bytes 24584 | tf_op jit(solution)/shard_map/ppermute | solution.py:33
  68.4 2.2 %collective-permute-start.6 = (f32[8,256]{1,0:T(8,128)S(1)}, f32[8,256]{1,0:T(8,128)S(1)}, u32[]{:S(2)}, u32[]{:S(2)}) collective-permute-start(f32[8,256]{1,0:T(8,128)S(1)} %get-tuple-element.40), channel_id=1, source_target_pairs={{0,0},{1,2},{2,1},{3,4},{4,3},{5,6},{6,5},{7,7},{8,8},{9,10},{10,9... | collective-permute-start | bytes 24584 | tf_op jit(solution)/shard_map/ppermute | solution.py:33
  71.8 2.9 %collective-permute-start.7 = (f32[4,8,256]{2,1,0:T(8,128)S(1)}, f32[4,8,256]{2,1,0:T(8,128)S(1)}, u32[]{:S(2)}, u32[]{:S(2)}) collective-permute-start(f32[4,8,256]{2,1,0:T(8,128)S(1)} %get-tuple-element.44), channel_id=1, source_target_pairs={{0,8},{8,0},{16,24},{24,16},{32,40},{40,32},{48,56},{56,48},{64,72... | collective-permute-start | bytes 98312 | tf_op jit(solution)/shard_map/ppermute | solution.py:33
  72.0 2.8 %collective-permute-start.8 = (f32[4,8,256]{2,1,0:T(8,128)S(1)}, f32[4,8,256]{2,1,0:T(8,128)S(1)}, u32[]{:S(2)}, u32[]{:S(2)}) collective-permute-start(f32[4,8,256]{2,1,0:T(8,128)S(1)} %get-tuple-element.45), channel_id=1, source_target_pairs={{0,0},{8,16},{16,8},{24,32},{32,24},{40,48},{48,40},{56,64},{64,56... | collective-permute-start | bytes 98312 | tf_op jit(solution)/shard_map/ppermute | solution.py:33
  79.8 3.8 %collective-permute-start.9 = (f32[128,3,128]{0,2,1:T(8,128)S(1)}, f32[128,3,128]{0,2,1:T(8,128)S(1)}, u32[]{:S(2)}, u32[]{:S(2)}) collective-permute-start(f32[128,3,128]{0,2,1:T(8,128)S(1)} %pad_maximum_fusion), channel_id=1, source_target_pairs={{0,128},{128,0},{1,129},{129,1},{2,130},{130,2},{3,131},{131,3},{4... | collective-permute-start | bytes 589832 | tf_op jit(solution)/shard_map/ppermute | solution.py:24
  113.6 2.9 %collective-permute-start.10 = (f32[24,256]{1,0:T(8,128)S(1)}, f32[24,256]{1,0:T(8,128)S(1)}, u32[]{:S(2)}, u32[]{:S(2)}) collective-permute-start(f32[24,256]{1,0:T(8,128)S(1)} %scatter.1), channel_id=1, source_target_pairs={{0,128},{128,0},{1,129},{129,1},{2,130},{130,2},{3,131},{131,3},{4... | collective-permute-start | bytes 73736 | tf_op jit(solution)/shard_map/ppermute | solution.py:24
